TPU v7x, 256 devices: a whole 4x4x8 slice. The times are simulated.
256 devices in a mesh: sec: 8 (over y, core), proto: 32 (over z, x).
Axes of the slice: x: 4, y: 4, z: 8, core: 2. Of those that a mesh axis runs over, the one named last changes fastest.
Arguments:
- features: bfloat16 [4096, 512], P('sec'), may hold values from -700 to 700
- prototypes: bfloat16 [512, 262144], P(None, 'proto'), may hold values from -20 to 20
- crop_sample: int32 [4096], P('sec'), may hold values from 0 to 1023, as said below
- crop_live: int32 [4096], P('sec'), may hold values 0 or 1
Outputs:
- crop_loss: float32 [4096], P('sec')
- embed_grad: float32 [4096, 512], P(('sec', 'proto'))
Inputs may be any that keep to these rules, and one draw needn't show every extreme that they name: `crop_sample`: on student rows the index of a teacher row, 0 to 1023; the entries on teacher rows are not read.
All inputs are finite; a program needn't handle non-finite values. No bound on the sum of `crop_live` on one device may be relied on, other than what follows from the above.
Results may differ from a plain program's by a relative error of at most 0.0067.
Values may be sent and summed in bfloat16 or wider, within the bound.
No kernel may reach another device: no remote copies, remote signals or barrier semaphores. Data moves between devices by JAX's collectives and lax.ppermute only.
A program may use at most 192 MiB of HBM per device.

v0:
```python
import functools

import jax
import jax.numpy as jnp
from jax import lax
from jax.experimental import pallas as pl
from jax.experimental.pallas import tpu as pltpu
from jax.sharding import PartitionSpec as P

PROTOS = 262144
SAMPLES = 1024
TEACH_TEMP = 0.07
STUD_TEMP = 0.1

F32 = jnp.float32
BF16 = jnp.bfloat16
LANES = 128
SUBS = 8

TEACH_A = 3
TEACH_B = 4

def is_teacher():
    sec = lax.axis_index("sec")
    return jnp.logical_or(sec == TEACH_A, sec == TEACH_B)


def row_to_column(row):
    return jnp.transpose(jnp.broadcast_to(row, (LANES, row.shape[1])))


def lanes_to_row(acc, reduce):
    return reduce(jnp.transpose(acc), axis=0, keepdims=True)


def pack_row(row):
    return jnp.concatenate(
        [row[:, i * LANES : (i + 1) * LANES] for i in range(row.shape[1] // LANES)], axis=0
    )


def unpack_row(packed):
    return jnp.concatenate([packed[i : i + 1, :] for i in range(packed.shape[0])], axis=1)


def tile_lanes(column, count):
    return jnp.concatenate([column] * count, axis=1)


def split_high(x):
    high = x.astype(BF16).astype(F32)
    return high, x - high


def write_parts(send_ref, product, rows):
    parts, each, _ = send_ref.shape
    width = product.shape[1]
    send_ref[:, :, :width] = product.astype(BF16).reshape(parts, each, width)
    extra = jnp.concatenate(rows, axis=0).astype(BF16)
    send_ref[:, :, width:] = jnp.broadcast_to(extra[None], (parts, each, LANES))


def send_copies(ref, packed):
    ref[...] = jnp.broadcast_to(packed[None], ref.shape)


def fold_lanes(op, block):
    out = block[:, :LANES]
    for i in range(1, block.shape[1] // LANES):
        out = op(out, block[:, i * LANES : (i + 1) * LANES])
    return out


def start_stream(w_hbm, w_ref, sems):
    chunk = w_ref.shape[1] // sems.shape[0]
    for j in range(sems.shape[0]):
        at = pl.ds(j * chunk, chunk)
        pltpu.make_async_copy(w_hbm.at[:, at], w_ref.at[:, at], sems.at[j]).start()


def wait_stream(w_hbm, w_ref, sems, j):
    chunk = w_ref.shape[1] // sems.shape[0]
    at = pl.ds(pl.multiple_of(j * chunk, chunk), chunk)
    pltpu.make_async_copy(w_hbm.at[:, at], w_ref.at[:, at], sems.at[j]).wait()


def unit_rows(features):
    values = features.astype(F32)
    total = jnp.sum(values * values, axis=1, keepdims=True)
    return (values * lax.rsqrt(total + 1e-06)).astype(BF16)


def logits_into(lhs_ref, w_ref, out_ref, top_ref, scale, wait=None, chunk=512):
    cols = w_ref.shape[1]
    top_ref[...] = jnp.full(top_ref.shape, -jnp.inf, F32)

    def step(j, carry):
        if wait is not None:
            wait(j)
        at = pl.ds(pl.multiple_of(j * chunk, chunk), chunk)
        z = jnp.dot(lhs_ref[...], w_ref[:, at], preferred_element_type=F32) * scale
        out_ref[:, at] = z
        top_ref[...] = jnp.maximum(top_ref[...], fold_lanes(jnp.maximum, z))
        return carry

    lax.fori_loop(0, cols // chunk, step, 0)


def column_sums(e_ref, weight_ref, put, width=512, block=64):
    rows, cols = e_ref.shape

    def step(j, carry):
        at = pl.ds(pl.multiple_of(j * width, width), width)

        def inner(i, acc):
            r = pl.ds(pl.multiple_of(i * block, block), block)
            x = e_ref[r, at] * tile_lanes(weight_ref[r, :], width // LANES)
            return acc + jnp.sum(x.reshape(block // SUBS, SUBS, width), axis=0)

        acc = lax.fori_loop(0, rows // block, inner, jnp.zeros((SUBS, width), F32))
        put(at, jnp.sum(acc, axis=0, keepdims=True))
        return carry

    lax.fori_loop(0, cols // width, step, 0)


def row_sums(e_ref, scale_ref, acc_ref, block=64, width=1024):
    rows, cols = e_ref.shape

    def step(i, carry):
        r = pl.ds(pl.multiple_of(i * block, block), block)

        def inner(j, acc):
            at = pl.ds(pl.multiple_of(j * width, width), width)
            x = e_ref[r, at] * scale_ref[:, at]
            return acc + fold_lanes(jnp.add, x)

        acc_ref[r, :] = lax.fori_loop(0, cols // width, inner, jnp.zeros((block, LANES), F32))
        return carry

    lax.fori_loop(0, rows // block, step, 0)


def first_logits(x_ref, w_hbm, l_ref, u_ref, send_ref, top_ref, w_ref, sems, *, scale):
    start_stream(w_hbm, w_ref, sems)
    u_ref[...] = unit_rows(x_ref[...])

    def wait(j):
        wait_stream(w_hbm, w_ref, sems, j)

    logits_into(u_ref, w_ref, l_ref, top_ref, scale, wait)
    packed = pack_row(lanes_to_row(top_ref[...], jnp.max))
    if len(send_ref.shape) == 3:
        send_copies(send_ref, packed)
    else:
        send_ref[...] = packed


def teacher_exponentials(l_ref, got_ref, e_ref, col_ref, top_ref, *, width=512, block=64):
    top_ref[...] = row_to_column(unpack_row(jnp.max(got_ref[...], axis=0)))
    rows, cols = e_ref.shape

    def step(j, carry):
        at = pl.ds(pl.multiple_of(j * width, width), width)

        def inner(i, acc):
            r = pl.ds(pl.multiple_of(i * block, block), block)
            x = jnp.exp(l_ref[r, at] - tile_lanes(top_ref[r, :], width // LANES))
            e_ref[r, at] = x
            return acc + jnp.sum(x.reshape(block // SUBS, SUBS, width), axis=0)

        acc = lax.fori_loop(0, rows // block, inner, jnp.zeros((SUBS, width), F32))
        col_ref[:, at] = jnp.sum(acc, axis=0, keepdims=True)
        return carry

    lax.fori_loop(0, cols // width, step, 0)


def teacher_rows(e_ref, own_ref, peer_ref, send_ref, scale_ref, acc_ref):
    scale_ref[...] = 1.0 / (PROTOS * (own_ref[...] + peer_ref[...]))
    row_sums(e_ref, scale_ref, acc_ref)
    send_copies(send_ref, pack_row(lanes_to_row(acc_ref[...], jnp.sum)))


def teacher_columns(e_ref, got_ref, col_ref, weight_ref):
    total = unpack_row(jnp.sum(got_ref[...], axis=0))
    weight_ref[...] = row_to_column(1.0 / (SAMPLES * total))

    def put(at, sums):
        col_ref[:, at] = sums

    column_sums(e_ref, weight_ref, put)


def teacher_last(e_ref, got_ref, top_ref, col_ref, weight_ref):
    total = unpack_row(jnp.sum(got_ref[...], axis=0))
    weight_ref[...] = row_to_column(1.0 / (SAMPLES * total))
    top = unpack_row(jnp.max(top_ref[...], axis=0))

    def put(at, sums):
        for s in range(col_ref.shape[0]):
            col_ref[s, :, at] = sums

    column_sums(e_ref, weight_ref, put)
    for s in range(col_ref.shape[0]):
        col_ref[s, :, e_ref.shape[1] :] = top


def student_product(
    l_ref, top_ref, w_hbm, send_ref, acc_ref, sum_ref, w_ref, sems
):
    start_stream(w_hbm, w_ref, sems)
    chunk = w_ref.shape[1] // sems.shape[0]
    packed = top_ref[...].astype(BF16).astype(F32)
    top = row_to_column(unpack_row(packed))
    acc_ref[...] = jnp.zeros_like(acc_ref)
    sum_ref[...] = jnp.zeros_like(sum_ref)

    def step(j, carry):
        at = pl.ds(pl.multiple_of(j * chunk, chunk), chunk)
        x = jnp.exp(l_ref[:, at] - tile_lanes(top, chunk // LANES))
        sum_ref[...] += fold_lanes(jnp.add, x)
        wait_stream(w_hbm, w_ref, sems, j)
        acc_ref[...] += lax.dot_general(
            x.astype(BF16), w_ref[:, at], (((1,), (1,)), ((), ())), preferred_element_type=F32
        )
        return carry

    lax.fori_loop(0, sems.shape[0], step, 0)
    high, low = split_high(pack_row(lanes_to_row(sum_ref[...], jnp.sum)))
    write_parts(send_ref, acc_ref[...], [packed, high, low, jnp.zeros_like(low)])


def stack_rows(p1_ref, p2_ref, both_ref):
    low = lax.axis_index("sec") < lax.axis_size("sec") // 2
    half = p1_ref.shape[0]

    @pl.when(low)
    def _():
        both_ref[:half, :] = p1_ref[...]
        both_ref[half:, :] = p2_ref[...]

    @pl.when(jnp.logical_not(low))
    def _():
        both_ref[:half, :] = p2_ref[...]
        both_ref[half:, :] = p1_ref[...]


def crop_first(
    w_hbm, index_ref, both_ref, p3_ref, p4_ref, ec_ref, send_ref, top_ref, crop_ref, rows_ref,
    w_ref, lc_ref, sems,
):
    start_stream(w_hbm, w_ref, sems)
    sec = lax.axis_index("sec")

    @pl.when(jnp.logical_or(sec == 2, sec == 5))
    def _():
        rows_ref[...] = both_ref[...]

    @pl.when(jnp.logical_or(sec == 0, sec == 7))
    def _():
        rows_ref[...] = p3_ref[...]

    @pl.when(jnp.logical_or(sec == 1, sec == 6))
    def _():
        rows_ref[...] = p4_ref[...]

    index = row_to_column(unpack_row(index_ref[...]))
    picked = jnp.zeros(crop_ref.shape, F32)
    for start in range(0, rows_ref.shape[0], 512):
        lane = lax.broadcasted_iota(jnp.int32, (index.shape[0], 512), 1) + start
        hot = jnp.where(tile_lanes(index, 4) == lane, 1.0, 0.0).astype(BF16)
        picked += jnp.dot(hot, rows_ref[start : start + 512, :], preferred_element_type=F32)
    crop_ref[...] = unit_rows(picked)

    def wait(j):
        wait_stream(w_hbm, w_ref, sems, j)

    logits_into(crop_ref, w_ref, lc_ref, top_ref, 1.0 / TEACH_TEMP, wait)
    row = lanes_to_row(top_ref[...], jnp.max)
    send_ref[...] = pack_row(row)
    top_ref[...] = row_to_column(row)
    width, block = 512, 64

    def outer(j, carry):
        at = pl.ds(pl.multiple_of(j * width, width), width)

        def inner(i, carry):
            r = pl.ds(pl.multiple_of(i * block, block), block)
            x = jnp.exp(lc_ref[r, at] - tile_lanes(top_ref[r, :], width // LANES))
            ec_ref[r, at] = x.astype(BF16)
            return carry

        return lax.fori_loop(0, lc_ref.shape[0] // block, inner, carry)

    lax.fori_loop(0, lc_ref.shape[1] // width, outer, 0)


def crop_product(
    ec_ref, cols_ref, w_ref, u_ref, index_ref, top_ref, send_ref, c_ref, acc_ref, fix_ref,
    *, chunk=1024,
):
    rows, cols = ec_ref.shape
    index = row_to_column(unpack_row(index_ref[...]))
    lane = lax.broadcasted_iota(jnp.int32, index.shape, 1)
    picked = jnp.zeros(index.shape, F32)
    for s, owner in enumerate((TEACH_A, TEACH_B)):
        for t in range(rows // LANES):
            tops = cols_ref[owner, :, cols + t * LANES : cols + (t + 1) * LANES]
            picked = jnp.where(index == lane + (s * rows + t * LANES), tops, picked)
    picked = jnp.sum(picked, axis=1, keepdims=True)
    fix_ref[...] = jnp.exp(row_to_column(unpack_row(top_ref[...])) - picked)
    c_ref[...] = jnp.zeros_like(c_ref)
    acc_ref[...] = jnp.zeros_like(acc_ref)

    def step(j, carry):
        at = pl.ds(pl.multiple_of(j * chunk, chunk), chunk)
        scale = 1.0 / (PROTOS * (cols_ref[TEACH_A, :, at] + cols_ref[TEACH_B, :, at]))
        y = ec_ref[:, at].astype(F32) * tile_lanes(fix_ref[...], chunk // LANES) * scale
        acc_ref[...] += fold_lanes(jnp.add, y)
        c_ref[...] += lax.dot_general(
            y.astype(BF16), w_ref[:, at], (((1,), (1,)), ((), ())), preferred_element_type=F32
        )
        return carry

    lax.fori_loop(0, cols // chunk, step, 0)
    cross = fold_lanes(jnp.add, u_ref[...].astype(F32) * c_ref[...]) * (1.0 / STUD_TEMP)
    total = split_high(pack_row(lanes_to_row(acc_ref[...], jnp.sum)))
    cross = split_high(pack_row(lanes_to_row(cross, jnp.sum)))
    write_parts(send_ref, c_ref[...], [*total, *cross])


def finish(a_ref, c_ref, live_ref, grad_ref, loss_ref, weight_ref, stud_ref, targ_ref):
    each, width = grad_ref.shape
    packs = live_ref.shape[0]
    teacher = is_teacher()

    @pl.when(teacher)
    def _():
        grad_ref[...] = jnp.zeros_like(grad_ref)
        loss_ref[...] = jnp.zeros_like(loss_ref)

    @pl.when(jnp.logical_not(teacher))
    def _():
        parts = a_ref.shape[0]
        extra = a_ref[:, :, width:].astype(F32)
        tops = extra[:, :packs]
        top = jnp.max(tops, axis=0)
        weight = jnp.exp(tops - top[None])
        sums = extra[:, packs : 2 * packs] + extra[:, 2 * packs : 3 * packs]
        total = jnp.sum(weight * sums, axis=0)
        rest = jnp.zeros((LANES - parts, LANES), F32)
        for i in range(packs):
            piece = jnp.concatenate([weight[:, i, :], rest], axis=0)
            weight_ref[i * LANES : (i + 1) * LANES, :] = jnp.transpose(piece)
        extra = jnp.sum(c_ref[:, :, width:].astype(F32), axis=0)
        target_sum = extra[:packs] + extra[packs : 2 * packs]
        cross = extra[2 * packs : 3 * packs] + extra[3 * packs :]
        live = live_ref[...].astype(F32)
        loss_ref[...] = live * (top + jnp.log(total) - cross / target_sum)
        scale = live * (1.0 / STUD_TEMP)
        stud_ref[...] = row_to_column(unpack_row(scale / total))
        targ_ref[...] = row_to_column(unpack_row(scale / target_sum))
        mine = pl.ds(pl.multiple_of(lax.axis_index("proto") * each, each), each)
        tiles = width // LANES
        factor = weight_ref[mine, :]
        stud = jnp.zeros(grad_ref.shape, F32)
        for p in range(parts):
            stud += a_ref[p, :, :width].astype(F32) * factor[:, p : p + 1]
        targ = jnp.sum(c_ref[:, :, :width].astype(F32), axis=0)
        grad_ref[...] = stud * tile_lanes(stud_ref[mine, :], tiles) - targ * tile_lanes(
            targ_ref[mine, :], tiles
        )


def relay(x_ref, y_ref):
    y_ref[...] = x_ref[...]


def hollow(*refs):
    pass


MIB = 2**20
HBM = pltpu.HBM
VMEM = pltpu.VMEM


def call(
    kernel, out, args, scratch=(), alias=None, flops=0, moved=0, limit=8, spaces=None, name=None,
    out_space=VMEM,
):
    spaces = spaces or [VMEM] * len(args)
    return pl.pallas_call(
        kernel,
        name=name or kernel.__name__,
        out_shape=tuple(jax.ShapeDtypeStruct(s, d) for s, d in out),
        in_specs=[pl.BlockSpec(memory_space=s) for s in spaces],
        out_specs=tuple([pl.BlockSpec(memory_space=out_space)] * len(out)),
        scratch_shapes=list(scratch),
        input_output_aliases=alias or {},
        cost_estimate=pl.CostEstimate(flops=flops, bytes_accessed=moved, transcendentals=0),
        compiler_params=pltpu.CompilerParams(vmem_limit_bytes=limit * MIB),
    )(*args)


def per_device(features, prototypes, crop_sample, crop_live):
    rows, width = features.shape
    cols = prototypes.shape[1]
    protos = lax.axis_size("proto")
    secs = lax.axis_size("sec")
    packs = rows // LANES
    each = rows // protos
    row_send = ((protos, packs, LANES), F32)
    one_row = ((packs, LANES), F32)
    parts = ((protos, each, width + LANES), BF16)
    column = ((1, cols), F32)
    columns = ((secs, 1, cols + rows), F32)
    table = ((rows, cols), F32)
    crop_table = ((rows, cols), BF16)
    units = ((rows, width), BF16)
    both_rows = ((2 * rows, width), BF16)
    lanes = VMEM((rows, LANES), F32)
    product = VMEM((rows, width), F32)
    line = VMEM((1, cols), F32)
    protos_vmem = VMEM((width, cols), BF16)
    big = rows * cols * 4
    gemm = 2 * rows * cols * width
    index = crop_sample.reshape(packs, LANES)
    live = crop_live.reshape(packs, LANES)
    pair = [(TEACH_A, TEACH_B), (TEACH_B, TEACH_A)]

    def sems(count):
        return pltpu.SemaphoreType.DMA((count,))

    def spread(x):
        return lax.all_to_all(x, "proto", 0, 0, tiled=True)

    def unused(after, *out):
        return call(hollow, out, [after], spaces=[pl.ANY], out_space=pl.ANY)

    def start(temp, send):
        return call(
            functools.partial(first_logits, scale=1.0 / temp),
            [table, units, send],
            [features, prototypes],
            [lanes, protos_vmem, sems(16)],
            flops=gemm, moved=big, spaces=[VMEM, HBM], limit=32, name="first_logits",
        )

    def teacher(p1):
        logits, _, send = start(TEACH_TEMP, row_send)
        top_got = spread(send)
        expo, col = call(
            teacher_exponentials, [table, column], [logits, top_got], [lanes], {0: 0},
            flops=big, moved=big,
        )
        for last in (False, True):
            peer = lax.ppermute(col, "sec", pair)
            (send,) = call(
                teacher_rows, [row_send], [expo, col, peer], [line, lanes], flops=big, moved=big
            )
            got = spread(send)
            if last:
                (col,) = call(
                    teacher_last, [columns], [expo, got, top_got], [lanes], flops=big, moved=big
                )
            else:
                (col,) = call(
                    teacher_columns, [column], [expo, got], [lanes], flops=big, moved=big
                )
        return col, *unused(col, crop_table, units, one_row, parts)

    def student(p1):
        p2 = lax.ppermute(p1, "sec", [(2, 5), (5, 2)])
        logits, unit, top = start(STUD_TEMP, one_row)
        top, p2 = lax.optimization_barrier((top, p2))
        (both,) = call(stack_rows, [both_rows], [p1, p2])
        p3 = lax.ppermute(both, "sec", [(2, 0), (5, 7)])
        (send,) = call(
            student_product, [parts], [logits, top, prototypes],
            [product, lanes, protos_vmem, sems(8)],
            flops=gemm, moved=big, spaces=[VMEM, VMEM, HBM], limit=32,
        )
        stud_got = spread(send)
        p3, stud_got = lax.optimization_barrier((p3, stud_got))
        p4 = lax.ppermute(p3, "sec", [(0, 1), (7, 6)])
        crop_expo, crop_top = call(
            crop_first,
            [crop_table, one_row],
            [prototypes, index, both, p3, p4],
            [lanes, VMEM(units[0], BF16), VMEM(both_rows[0], BF16), protos_vmem, VMEM(*table), sems(16)],
            flops=gemm, moved=big, spaces=[HBM] + [VMEM] * 4, limit=48,
        )
        return *unused(crop_expo, columns), crop_expo, unit, crop_top, stud_got

    p1 = lax.ppermute(features, "sec", [(3, 2), (4, 5)])
    col, expo, unit, crop_top, stud_got = lax.cond(is_teacher(), teacher, student, p1)
    (col,) = call(relay, [columns], [col], flops=gemm, moved=big)
    cols_got = lax.all_to_all(col, "sec", 0, 0, tiled=True)
    (send,) = call(
        crop_product,
        [parts],
        [expo, cols_got, prototypes, unit, index, crop_top],
        [product, lanes, lanes],
        flops=gemm, moved=big, limit=12,
    )
    grad, loss = call(
        finish,
        [((each, width), F32), ((packs, LANES), F32)],
        [stud_got, spread(send), live],
        [lanes, lanes, lanes],
    )
    return loss.reshape(rows), grad


def solution(mesh):
    in_specs = (P("sec", None), P(None, "proto"), P("sec"), P("sec"))
    out_specs = (P("sec"), P(("sec", "proto"), None))
    return jax.shard_map(
        per_device, mesh=mesh, in_specs=in_specs, out_specs=out_specs, check_vma=False
    )
```

profile of v0, /device:TPU:2, one launch (start us, length us, event | category | flops | bytes accessed | tf_op | source)
XLA Modules:
  0.0 130.1 jit_solution(12251507701699232805)
XLA Ops:
  0.6 0.7 collective-permute-start.5
  1.3 0.0 collective-permute-done.5
  1.4 70.6 %conditional.1 = (f32[8,1,8704]{2,1,0:T(1,128)}, bf16[512,8192]{1,0:T(8,128)(2,1)S(1)}, bf16[512,512]{1,0:T(8,128)(2,1)}, f32[4,128]{1,0:T(4,128)S(1)}, bf16[32,16,640]{2,1,0:T(8,128)(2,1)S(1)}) conditional(s32[]{:T(128)} %convert_element_type.3, (bf16[512,512]{1,0:T(8,128)(2,1)}, bf16[512,8192]{1,0:T(8,128)(2,1)}, bf16[512,512]{1,0:T(8,128)(2,1)S(1)}, ...), branch_computations={%region_0.0_spmd, %region_1.0_spmd} | conditional | flops 12884901888 | bytes 101318776 | solution.py:498
  1.4 0.0 slice-start.2
  1.4 0.8 collective-permute-start
  2.2 0.0 slice-start.3
  2.2 10.5 %first_logits.2 = (f32[512,8192]{1,0:T(8,128)S(1)}, bf16[512,512]{1,0:T(8,128)(2,1)}, f32[4,128]{1,0:T(4,128)S(1)}) custom-call(bf16[512,512]{1,0:T(8,128)(2,1)} %get-tuple-element.15.x_ref, bf16[512,8192]{1,0:T(8,128)(2,1)} %get-tuple-element.12.w_hbm), custom_call_target="tpu_custom_call" | custom-call | flops 4294967296 | bytes 16777216 | tf_op jit(solution)/shard_map/cond/branch_0_fun/first_logits/pallas_call | solution.py:394
  12.7 0.0 collective-permute-done.p2_ref
  12.7 0.0 slice-done.2
  12.7 0.0 slice-done.3
  12.7 0.0 copy-start.3
  12.7 10.6 %student_product.1 = bf16[32,16,640]{2,1,0:T(8,128)(2,1)} custom-call(f32[512,8192]{1,0:T(8,128)S(1)} %get-tuple-element.18.l_ref, f32[4,128]{1,0:T(4,128)S(1)} %get-tuple-element.19.top_ref, bf16[512,8192]{1,0:T(8,128)(2,1)S(1)} %bitcast.7), custom_call_target="tpu_custom_call" | custom-call | flops 4294967296 | bytes 16777216 | tf_op jit(solution)/shard_map/cond/branch_0_fun/student_product/pallas_call | solution.py:394
  23.4 11.6 %all-to-all-start = ((bf16[32,16,640]{2,1,0:T(8,128)(2,1)}), bf16[32,16,640]{2,1,0:T(8,128)(2,1)S(1)}, u32[]{:S(2)}, u32[]{:S(2)}) async-start(bf16[32,16,640]{2,1,0:T(8,128)(2,1)} %student_product.1), calls=%async_computation | async-start | bytes 1310720 | tf_op jit(solution)/shard_map/cond/branch_0_fun/all_to_all | solution.py:437
  35.0 0.1 stack_rows.1.both_ref
  35.1 1.3 collective-permute-start.1
  36.4 19.6 %collective-permute-done.1.p3_ref = bf16[1024,512]{1,0:T(8,128)(2,1)S(1)} collective-permute-done((bf16[1024,512]{1,0:T(8,128)(2,1)S(1)}, bf16[1024,512]{1,0:T(8,128)(2,1)S(1)}, u32[]{:S(2)}, u32[]{:S(2)}) %collective-permute-start.1) | collective-permute-done | bytes 1048608 | tf_op jit(solution)/shard_map/cond/branch_0_fun/ppermute | solution.py:479
  56.0 0.0 all-to-all-done
  56.0 1.3 %collective-permute-start.2 = (bf16[1024,512]{1,0:T(8,128)(2,1)S(1)}, bf16[1024,512]{1,0:T(8,128)(2,1)S(1)}, u32[]{:S(2)}, u32[]{:S(2)}) collective-permute-start(bf16[1024,512]{1,0:T(8,128)(2,1)S(1)} %collective-permute-done.1.p3_ref), channel_id=1, source_target_pairs={{0,32},{224,192},{1,33},{225,193},{2,34},{226,194},{3,35},{227,195... | collective-permute-start | bytes 3145736 | tf_op jit(solution)/shard_map/cond/branch_0_fun/ppermute | solution.py:487
  57.4 2.2 %collective-permute-done.2.p4_ref = bf16[1024,512]{1,0:T(8,128)(2,1)S(1)} collective-permute-done((bf16[1024,512]{1,0:T(8,128)(2,1)S(1)}, bf16[1024,512]{1,0:T(8,128)(2,1)S(1)}, u32[]{:S(2)}, u32[]{:S(2)}) %collective-permute-start.2) | collective-permute-done | bytes 1048608 | tf_op jit(solution)/shard_map/cond/branch_0_fun/ppermute | solution.py:487
  59.6 0.0 copy-done.3
  59.6 12.4 %crop_first.1 = (bf16[512,8192]{1,0:T(8,128)(2,1)S(1)}, f32[4,128]{1,0:T(4,128)S(1)}) custom-call(bf16[512,8192]{1,0:T(8,128)(2,1)} %get-tuple-element.12.w_hbm, s32[4,128]{1,0:T(4,128)S(1)} %copy-done.3, bf16[1024,512]{1,0:T(8,128)(2,1)S(1)} %stack_rows.1.both_ref, bf16[1024,512]{1,0:T(8,128)(2,1)S(1)} %collective-permute-done.1.p3_ref, ...), custom_call_target="tpu_custom_call" | custom-call | flops 4294967296 | bytes 16777216 | tf_op jit(solution)/shard_map/cond/branch_0_fun/crop_first/pallas_call | solution.py:394
  72.0 0.0 slice-start
  72.0 0.0 copy-start.1
  72.0 0.0 copy-start.2
  72.0 0.0 slice-start.1
  72.0 1.1 relay.1
  73.2 24.6 %all_to_all.29.cols_ref = f32[8,1,8704]{2,1,0:T(1,128)S(1)} all-to-all(f32[8,1,8704]{2,1,0:T(1,128)S(1)} %relay.1), channel_id=1, replica_groups=mesh['sec'=8,'proto'=32] {'sec'}, dimensions={0} | all-to-all | bytes 557056 | tf_op jit(solution)/shard_map/all_to_all | solution.py:500
  97.7 0.0 slice-done
  97.8 0.0 copy-done.1
  97.8 0.0 copy-done.2
  97.8 0.0 slice-done.1
  97.8 0.0 copy-start
  97.8 6.9 %crop_product.1 = bf16[32,16,640]{2,1,0:T(8,128)(2,1)S(1)} custom-call(bf16[512,8192]{1,0:T(8,128)(2,1)S(1)} %get-tuple-element.45.ec_ref, f32[8,1,8704]{2,1,0:T(1,128)S(1)} %all_to_all.29.cols_ref, bf16[512,8192]{1,0:T(8,128)(2,1)S(1)} %bitcast.5, bf16[512,512]{1,0:T(8,128)(2,1)S(1)} %copy-done.1, s32[4,128]{1,0:T(4,128)S(1)} %bitcast.9, ...), custom_call_target="tpu_custom_call" | custom-call | flops 4294967296 | bytes 16777216 | tf_op jit(solution)/shard_map/crop_product/pallas_call | solution.py:394
  104.7 24.3 %all_to_all.30.c_ref = bf16[32,16,640]{2,1,0:T(8,128)(2,1)S(1)} all-to-all(bf16[32,16,640]{2,1,0:T(8,128)(2,1)S(1)} %crop_product.1), channel_id=1, replica_groups=mesh['sec'=8,'proto'=32] {'proto'}, dimensions={0} | all-to-all | bytes 1310720 | tf_op jit(solution)/shard_map/all_to_all | solution.py:437
  129.0 0.0 copy-done
  129.0 1.1 finish.1
  (3 shorter events, 0.0 us)
Async XLA Ops:
  0.6 0.7 collective-permute-start.5
  1.4 11.3 %slice-start.2 = ((s8[8388608]{0:T(1024)(128)(4,1)}), s8[4194304]{0:T(1024)(128)(4,1)S(1)}, s32[]{:S(2)}) async-start(s8[8388608]{0:T(1024)(128)(4,1)} %bitcast.6), calls=%async_computation.8 | async-start | bytes 8388608 | tf_op jit(solution)/shard_map/cond
  1.4 11.3 %collective-permute-start = (bf16[512,512]{1,0:T(8,128)(2,1)S(1)}, bf16[512,512]{1,0:T(8,128)(2,1)S(1)}, u32[]{:S(2)}, u32[]{:S(2)}) collective-permute-start(bf16[512,512]{1,0:T(8,128)(2,1)S(1)} %get-tuple-element.14.p1_ref), channel_id=1, source_target_pairs={{64,160},{160,64},{65,161},{161,65},{66,162},{162,66},{67,163},{16... | collective-permute-start | bytes 1572872 | tf_op jit(solution)/shard_map/cond/branch_0_fun/ppermute | solution.py:475
  2.2 10.5 %slice-start.3 = ((s8[8388608]{0:T(1024)(128)(4,1)}), s8[4194304]{0:T(1024)(128)(4,1)S(1)}, s32[]{:S(2)}) async-start(s8[8388608]{0:T(1024)(128)(4,1)} %bitcast.6), calls=%async_computation.9 | async-start | bytes 8388608 | tf_op jit(solution)/shard_map/cond
  12.7 46.8 %copy-start.3 = (s32[4,128]{1,0:T(4,128)S(1)}, s32[4,128]{1,0:T(4,128)}, u32[]{:S(2)}) copy-start(s32[4,128]{1,0:T(4,128)} %get-tuple-element.13.index_ref) | copy-start | bytes 6148 | tf_op jit(solution)/shard_map/cond
  23.4 32.6 %all-to-all-start = ((bf16[32,16,640]{2,1,0:T(8,128)(2,1)}), bf16[32,16,640]{2,1,0:T(8,128)(2,1)S(1)}, u32[]{:S(2)}, u32[]{:S(2)}) async-start(bf16[32,16,640]{2,1,0:T(8,128)(2,1)} %student_product.1), calls=%async_computation | async-start | bytes 1310720 | tf_op jit(solution)/shard_map/cond/branch_0_fun/all_to_all | solution.py:437
  35.1 20.9 %collective-permute-start.1 = (bf16[1024,512]{1,0:T(8,128)(2,1)S(1)}, bf16[1024,512]{1,0:T(8,128)(2,1)S(1)}, u32[]{:S(2)}, u32[]{:S(2)}) collective-permute-start(bf16[1024,512]{1,0:T(8,128)(2,1)S(1)} %stack_rows.1.both_ref), channel_id=1, source_target_pairs={{64,0},{160,224},{65,1},{161,225},{66,2},{162,226},{67,3},{163,227... | collective-permute-start | bytes 3145736 | tf_op jit(solution)/shard_map/cond/branch_0_fun/ppermute | solution.py:479
  56.0 3.6 %collective-permute-start.2 = (bf16[1024,512]{1,0:T(8,128)(2,1)S(1)}, bf16[1024,512]{1,0:T(8,128)(2,1)S(1)}, u32[]{:S(2)}, u32[]{:S(2)}) collective-permute-start(bf16[1024,512]{1,0:T(8,128)(2,1)S(1)} %collective-permute-done.1.p3_ref), channel_id=1, source_target_pairs={{0,32},{224,192},{1,33},{225,193},{2,34},{226,194},{3,35},{227,195... | collective-permute-start | bytes 3145736 | tf_op jit(solution)/shard_map/cond/branch_0_fun/ppermute | solution.py:487
  72.0 25.8 %slice-start = ((s8[8388608]{0:T(1024)(128)(4,1)}), s8[4194304]{0:T(1024)(128)(4,1)S(1)}, s32[]{:S(2)}) async-start(s8[8388608]{0:T(1024)(128)(4,1)} %bitcast.4), calls=%async_computation.6 | async-start | bytes 8388608
  72.0 25.8 %copy-start.1 = (bf16[512,512]{1,0:T(8,128)(2,1)S(1)}, bf16[512,512]{1,0:T(8,128)(2,1)}, u32[]{:S(2)}) copy-start(bf16[512,512]{1,0:T(8,128)(2,1)} %get-tuple-element.47.u_ref) | copy-start | bytes 1572868
  72.0 25.7 %copy-start.2 = (s32[512]{0:T(512)S(1)}, s32[512]{0:T(512)}, u32[]{:S(2)}) copy-start(s32[512]{0:T(512)} %param.8) | copy-start | bytes 6148
  72.0 25.7 %slice-start.1 = ((s8[8388608]{0:T(1024)(128)(4,1)}), s8[4194304]{0:T(1024)(128)(4,1)S(1)}, s32[]{:S(2)}) async-start(s8[8388608]{0:T(1024)(128)(4,1)} %bitcast.4), calls=%async_computation.7 | async-start | bytes 8388608
  97.8 31.2 %copy-start = (s32[512]{0:T(512)S(1)}, s32[512]{0:T(512)}, u32[]{:S(2)}) copy-start(s32[512]{0:T(512)} %param.9) | copy-start | bytes 6148
where the time goes:
time: 130 us
  blocking collectives  48.9 us (38%)
  Pallas kernels  42.7 us (33%)
  waiting for transfers between devices  21.8 us (17%)
  starting transfers between devices  15.8 us (12%)
    pallas_call x8, Pallas kernels, call(): pl.pallas_call(kernel, name=name or kernel.__name__, out_shape=tuple((jax...  42.7 us
    all_to_all x1, blocking collectives, per_device(): cols_got = lax.all_to_all(col, 'sec', 0, 0, tiled=True)  24.6 us
    all_to_all x1, blocking collectives, spread(): return lax.all_to_all(x, 'proto', 0, 0, tiled=True)  24.3 us
    ppermute x1, waiting for transfers between devices, student(): p3 = lax.ppermute(both, 'sec', [(2, 0), (5, 7)])  19.6 us
    all_to_all x1, starting transfers between devices, spread(): return lax.all_to_all(x, 'proto', 0, 0, tiled=True)  11.6 us
  transfers between devices with their start and end apart: 5, of which 2 were waited for; matrix products, arithmetic and copies ran while one was open for 0% of the time, Pallas kernels for 8%

commit v1 on v0

--- a/solution.py
+++ b/solution.py
@@ -71,17 +71,22 @@
     return out
 
 
-def start_stream(w_hbm, w_ref, sems):
-    chunk = w_ref.shape[1] // sems.shape[0]
-    for j in range(sems.shape[0]):
-        at = pl.ds(j * chunk, chunk)
-        pltpu.make_async_copy(w_hbm.at[:, at], w_ref.at[:, at], sems.at[j]).start()
-
-
-def wait_stream(w_hbm, w_ref, sems, j):
+def block_copy(w_hbm, w_ref, sems, j):
     chunk = w_ref.shape[1] // sems.shape[0]
     at = pl.ds(pl.multiple_of(j * chunk, chunk), chunk)
-    pltpu.make_async_copy(w_hbm.at[:, at], w_ref.at[:, at], sems.at[j]).wait()
+    return pltpu.make_async_copy(w_hbm.at[:, at], w_ref.at[:, at], sems.at[j])
+
+
+def start_stream(w_hbm, w_ref, sems):
+    block_copy(w_hbm, w_ref, sems, 0).start()
+
+
+def wait_stream(w_hbm, w_ref, sems, j):
+    block_copy(w_hbm, w_ref, sems, j).wait()
+
+    @pl.when(j + 1 < sems.shape[0])
+    def _():
+        block_copy(w_hbm, w_ref, sems, j + 1).start()
 
 
 def unit_rows(features):
@@ -90,13 +95,12 @@
     return (values * lax.rsqrt(total + 1e-06)).astype(BF16)
 
 
-def logits_into(lhs_ref, w_ref, out_ref, top_ref, scale, wait=None, chunk=512):
+def logits_into(lhs_ref, w_ref, out_ref, top_ref, scale, wait, chunk):
     cols = w_ref.shape[1]
     top_ref[...] = jnp.full(top_ref.shape, -jnp.inf, F32)
 
     def step(j, carry):
-        if wait is not None:
-            wait(j)
+        wait(j)
         at = pl.ds(pl.multiple_of(j * chunk, chunk), chunk)
         z = jnp.dot(lhs_ref[...], w_ref[:, at], preferred_element_type=F32) * scale
         out_ref[:, at] = z
@@ -106,7 +110,7 @@
     lax.fori_loop(0, cols // chunk, step, 0)
 
 
-def column_sums(e_ref, weight_ref, put, width=512, block=64):
+def column_sums(e_ref, weight_ref, put, width=512, block=256):
     rows, cols = e_ref.shape
 
     def step(j, carry):
@@ -148,7 +152,7 @@
     def wait(j):
         wait_stream(w_hbm, w_ref, sems, j)
 
-    logits_into(u_ref, w_ref, l_ref, top_ref, scale, wait)
+    logits_into(u_ref, w_ref, l_ref, top_ref, scale, wait, w_ref.shape[1] // sems.shape[0])
     packed = pack_row(lanes_to_row(top_ref[...], jnp.max))
     if len(send_ref.shape) == 3:
         send_copies(send_ref, packed)
@@ -156,7 +160,7 @@
         send_ref[...] = packed
 
 
-def teacher_exponentials(l_ref, got_ref, e_ref, col_ref, top_ref, *, width=512, block=64):
+def teacher_exponentials(l_ref, got_ref, e_ref, col_ref, top_ref, *, width=512, block=256):
     top_ref[...] = row_to_column(unpack_row(jnp.max(got_ref[...], axis=0)))
     rows, cols = e_ref.shape
 
@@ -192,18 +196,22 @@
     column_sums(e_ref, weight_ref, put)
 
 
-def teacher_last(e_ref, got_ref, top_ref, col_ref, weight_ref):
+def teacher_last(e_ref, got_ref, top_ref, col_ref, weight_ref, line_ref):
     total = unpack_row(jnp.sum(got_ref[...], axis=0))
     weight_ref[...] = row_to_column(1.0 / (SAMPLES * total))
-    top = unpack_row(jnp.max(top_ref[...], axis=0))
+    secs, count, width = col_ref.shape
+    width -= LANES
 
     def put(at, sums):
-        for s in range(col_ref.shape[0]):
-            col_ref[s, :, at] = sums
+        line_ref[:, at] = sums
 
     column_sums(e_ref, weight_ref, put)
-    for s in range(col_ref.shape[0]):
-        col_ref[s, :, e_ref.shape[1] :] = top
+    rows = [line_ref[:, i * width : (i + 1) * width] for i in range(count)]
+    tops = jnp.max(top_ref[...], axis=0)
+    tops = jnp.concatenate([tops, jnp.zeros((count - tops.shape[0], LANES), F32)], axis=0)
+    full = jnp.concatenate([jnp.concatenate(rows, axis=0), tops], axis=1).astype(BF16)
+    for i in range(secs):
+        col_ref[i] = full
 
 
 def student_product(
@@ -276,7 +284,8 @@
     def wait(j):
         wait_stream(w_hbm, w_ref, sems, j)
 
-    logits_into(crop_ref, w_ref, lc_ref, top_ref, 1.0 / TEACH_TEMP, wait)
+    chunk = w_ref.shape[1] // sems.shape[0]
+    logits_into(crop_ref, w_ref, lc_ref, top_ref, 1.0 / TEACH_TEMP, wait, chunk)
     row = lanes_to_row(top_ref[...], jnp.max)
     send_ref[...] = pack_row(row)
     top_ref[...] = row_to_column(row)
@@ -298,15 +307,21 @@
 
 def crop_product(
     ec_ref, cols_ref, w_ref, u_ref, index_ref, top_ref, send_ref, c_ref, acc_ref, fix_ref,
-    *, chunk=1024,
+    scale_ref, *, chunk=2048,
 ):
     rows, cols = ec_ref.shape
+    _, count, size = cols_ref.shape
+    size -= LANES
+    first, second = cols_ref[TEACH_A].astype(F32), cols_ref[TEACH_B].astype(F32)
+    scale = 1.0 / (PROTOS * (first[:, :size] + second[:, :size]))
+    for i in range(count):
+        scale_ref[:, i * size : (i + 1) * size] = scale[i : i + 1]
     index = row_to_column(unpack_row(index_ref[...]))
     lane = lax.broadcasted_iota(jnp.int32, index.shape, 1)
     picked = jnp.zeros(index.shape, F32)
-    for s, owner in enumerate((TEACH_A, TEACH_B)):
+    for s, owner in enumerate((first, second)):
         for t in range(rows // LANES):
-            tops = cols_ref[owner, :, cols + t * LANES : cols + (t + 1) * LANES]
+            tops = owner[t : t + 1, size:]
             picked = jnp.where(index == lane + (s * rows + t * LANES), tops, picked)
     picked = jnp.sum(picked, axis=1, keepdims=True)
     fix_ref[...] = jnp.exp(row_to_column(unpack_row(top_ref[...])) - picked)
@@ -315,8 +330,7 @@
 
     def step(j, carry):
         at = pl.ds(pl.multiple_of(j * chunk, chunk), chunk)
-        scale = 1.0 / (PROTOS * (cols_ref[TEACH_A, :, at] + cols_ref[TEACH_B, :, at]))
-        y = ec_ref[:, at].astype(F32) * tile_lanes(fix_ref[...], chunk // LANES) * scale
+        y = ec_ref[:, at].astype(F32) * scale_ref[:, at]
         acc_ref[...] += fold_lanes(jnp.add, y)
         c_ref[...] += lax.dot_general(
             y.astype(BF16), w_ref[:, at], (((1,), (1,)), ((), ())), preferred_element_type=F32
@@ -324,8 +338,9 @@
         return carry
 
     lax.fori_loop(0, cols // chunk, step, 0)
+    c_ref[...] *= tile_lanes(fix_ref[...], c_ref.shape[1] // LANES)
     cross = fold_lanes(jnp.add, u_ref[...].astype(F32) * c_ref[...]) * (1.0 / STUD_TEMP)
-    total = split_high(pack_row(lanes_to_row(acc_ref[...], jnp.sum)))
+    total = split_high(pack_row(lanes_to_row(acc_ref[...] * fix_ref[...], jnp.sum)))
     cross = split_high(pack_row(lanes_to_row(cross, jnp.sum)))
     write_parts(send_ref, c_ref[...], [*total, *cross])
 
@@ -373,8 +388,10 @@
         )
 
 
-def relay(x_ref, y_ref):
-    y_ref[...] = x_ref[...]
+def fetch(w_hbm, w_ref, sem):
+    copy = pltpu.make_async_copy(w_hbm, w_ref, sem)
+    copy.start()
+    copy.wait()
 
 
 def hollow(*refs):
@@ -415,7 +432,7 @@
     one_row = ((packs, LANES), F32)
     parts = ((protos, each, width + LANES), BF16)
     column = ((1, cols), F32)
-    columns = ((secs, 1, cols + rows), F32)
+    columns = ((secs, 8, cols // 8 + LANES), BF16)
     table = ((rows, cols), F32)
     crop_table = ((rows, cols), BF16)
     units = ((rows, width), BF16)
@@ -444,7 +461,7 @@
             functools.partial(first_logits, scale=1.0 / temp),
             [table, units, send],
             [features, prototypes],
-            [lanes, protos_vmem, sems(16)],
+            [lanes, protos_vmem, sems(4)],
             flops=gemm, moved=big, spaces=[VMEM, HBM], limit=32, name="first_logits",
         )
 
@@ -463,13 +480,13 @@
             got = spread(send)
             if last:
                 (col,) = call(
-                    teacher_last, [columns], [expo, got, top_got], [lanes], flops=big, moved=big
+                    teacher_last, [columns], [expo, got, top_got], [lanes, line], flops=big, moved=big
                 )
             else:
                 (col,) = call(
                     teacher_columns, [column], [expo, got], [lanes], flops=big, moved=big
                 )
-        return col, *unused(col, crop_table, units, one_row, parts)
+        return col, *unused(col, crop_table, crop_table, units, one_row, parts)
 
     def student(p1):
         p2 = lax.ppermute(p1, "sec", [(2, 5), (5, 2)])
@@ -479,7 +496,7 @@
         p3 = lax.ppermute(both, "sec", [(2, 0), (5, 7)])
         (send,) = call(
             student_product, [parts], [logits, top, prototypes],
-            [product, lanes, protos_vmem, sems(8)],
+            [product, lanes, protos_vmem, sems(4)],
             flops=gemm, moved=big, spaces=[VMEM, VMEM, HBM], limit=32,
         )
         stud_got = spread(send)
@@ -489,21 +506,24 @@
             crop_first,
             [crop_table, one_row],
             [prototypes, index, both, p3, p4],
-            [lanes, VMEM(units[0], BF16), VMEM(both_rows[0], BF16), protos_vmem, VMEM(*table), sems(16)],
-            flops=gemm, moved=big, spaces=[HBM] + [VMEM] * 4, limit=48,
-        )
-        return *unused(crop_expo, columns), crop_expo, unit, crop_top, stud_got
+            [lanes, VMEM(units[0], BF16), VMEM(both_rows[0], BF16), protos_vmem, VMEM(*table), sems(4)],
+            flops=gemm, moved=big, spaces=[HBM] + [VMEM] * 4, limit=36,
+        )
+        (protos_here,) = call(
+            fetch, [crop_table], [prototypes], [pltpu.SemaphoreType.DMA],
+            flops=big, moved=big, spaces=[HBM],
+        )
+        return *unused(crop_expo, columns), crop_expo, protos_here, unit, crop_top, stud_got
 
     p1 = lax.ppermute(features, "sec", [(3, 2), (4, 5)])
-    col, expo, unit, crop_top, stud_got = lax.cond(is_teacher(), teacher, student, p1)
-    (col,) = call(relay, [columns], [col], flops=gemm, moved=big)
+    col, expo, protos_here, unit, crop_top, stud_got = lax.cond(is_teacher(), teacher, student, p1)
     cols_got = lax.all_to_all(col, "sec", 0, 0, tiled=True)
     (send,) = call(
         crop_product,
         [parts],
-        [expo, cols_got, prototypes, unit, index, crop_top],
-        [product, lanes, lanes],
-        flops=gemm, moved=big, limit=12,
+        [expo, cols_got, protos_here, unit, index, crop_top],
+        [product, lanes, lanes, line],
+        flops=gemm, moved=big, limit=24,
     )
     grad, loss = call(
         finish,

time: 130 us -> 124 us (0.954)
  blocking collectives: 48.9 us -> 44.7 us
  waiting for transfers between devices: 21.8 us -> 19.6 us
    all_to_all x1, blocking collectives: 24.6 us -> 20.8 us  [per_device(): cols_got = lax.all_to_all(col, 'sec', 0, 0, tiled=True)]
    ppermute x1, waiting for transfers between devices: 2.2 us -> 0.01 us  [student(): p4 = lax.ppermute(p3, 'sec', [(0, 1), (7, 6)])]
  transfers between devices with their start and end apart: 5 -> 5, of which waited for: 2 -> 1; matrix products, arithmetic and copies ran while one was open for 0% -> 0% of each run, Pallas kernels for 8% -> 11%
where the time goes in v1:
time: 124 us; the launch traced here: 123 us
  blocking collectives  44.7 us (36%)
  Pallas kernels  42.5 us (34%)
  waiting for transfers between devices  19.6 us (16%)
  starting transfers between devices  15.8 us (13%)
    pallas_call x8, Pallas kernels, call(): pl.pallas_call(kernel, name=name or kernel.__name__, out_shape=tuple((jax...  42.5 us
    all_to_all x1, blocking collectives, spread(): return lax.all_to_all(x, 'proto', 0, 0, tiled=True)  24 us
    all_to_all x1, blocking collectives, per_device(): cols_got = lax.all_to_all(col, 'sec', 0, 0, tiled=True)  20.8 us
    ppermute x1, waiting for transfers between devices, student(): p3 = lax.ppermute(both, 'sec', [(2, 0), (5, 7)])  19.6 us
    all_to_all x1, starting transfers between devices, spread(): return lax.all_to_all(x, 'proto', 0, 0, tiled=True)  11.6 us
  transfers between devices with their start and end apart: 5, of which 1 were waited for; matrix products, arithmetic and copies ran while one was open for 0% of the time, Pallas kernels for 11%

profile of v1, /device:TPU:2, one launch (start us, length us, event | category | flops | bytes accessed | tf_op | source)
XLA Modules:
  0.0 123.5 jit_solution(3686274666729230457)
XLA Ops:
  0.6 0.7 collective-permute-start.5
  1.3 0.0 collective-permute-done.5
  1.4 69.4 %conditional.1 = (bf16[8,8,1152]{2,1,0:T(8,128)(2,1)}, bf16[512,8192]{1,0:T(8,128)(2,1)S(1)}, bf16[512,8192]{1,0:T(8,128)(2,1)S(1)}, bf16[512,512]{1,0:T(8,128)(...) conditional(s32[]{:T(128)} %convert_element_type.3, (bf16[512,512]{1,0:T(8,128)(2,1)}, ...), branch_computations={%region_0.0_spmd, %region_1.0_spmd} | conditional | flops 12901679104 | bytes 104734992 | solution.py:519
  1.4 0.0 slice-start
  1.4 0.8 collective-permute-start
  2.2 0.0 slice-start.1
  2.2 9.6 %first_logits.2 = (f32[512,8192]{1,0:T(8,128)S(1)}, bf16[512,512]{1,0:T(8,128)(2,1)}, f32[4,128]{1,0:T(4,128)S(1)}) custom-call(bf16[512,512]{1,0:T(8,128)(2,1)} %get-tuple-element.15.x_ref, bf16[512,8192]{1,0:T(8,128)(2,1)} %get-tuple-element.12.w_hbm), custom_call_target="tpu_custom_call" | custom-call | flops 4294967296 | bytes 16777216 | tf_op jit(solution)/shard_map/cond/branch_0_fun/first_logits/pallas_call | solution.py:411
  11.8 0.0 collective-permute-done.p2_ref
  11.8 0.0 slice-done
  11.8 0.0 slice-done.1
  11.8 9.7 %student_product.1 = bf16[32,16,640]{2,1,0:T(8,128)(2,1)} custom-call(f32[512,8192]{1,0:T(8,128)S(1)} %get-tuple-element.18.l_ref, f32[4,128]{1,0:T(4,128)S(1)} %get-tuple-element.19.top_ref, bf16[512,8192]{1,0:T(8,128)(2,1)S(1)} %bitcast.5), custom_call_target="tpu_custom_call" | custom-call | flops 4294967296 | bytes 16777216 | tf_op jit(solution)/shard_map/cond/branch_0_fun/student_product/pallas_call | solution.py:411
  21.5 11.6 %all-to-all-start = ((bf16[32,16,640]{2,1,0:T(8,128)(2,1)}), bf16[32,16,640]{2,1,0:T(8,128)(2,1)S(1)}, u32[]{:S(2)}, u32[]{:S(2)}) async-start(bf16[32,16,640]{2,1,0:T(8,128)(2,1)} %student_product.1), calls=%async_computation | async-start | bytes 1310720 | tf_op jit(solution)/shard_map/cond/branch_0_fun/all_to_all | solution.py:454
  33.2 0.1 stack_rows.1.both_ref
  33.3 0.0 copy-start.1
  33.3 1.3 %collective-permute-start.1 = (bf16[1024,512]{1,0:T(8,128)(2,1)S(1)}, bf16[1024,512]{1,0:T(8,128)(2,1)S(1)}, u32[]{:S(2)}, u32[]{:S(2)}) collective-permute-start(bf16[1024,512]{1,0:T(8,128)(2,1)S(1)} %stack_rows.1.both_ref), channel_id=1, source_target_pairs={{64,0},{160,224},{65,1},{161,225},{66,2},{162,226},{67,3},{163,227... | collective-permute-start | bytes 3145736 | tf_op jit(solution)/shard_map/cond/branch_0_fun/ppermute | solution.py:496
  34.6 19.6 %collective-permute-done.1.p3_ref = bf16[1024,512]{1,0:T(8,128)(2,1)S(1)} collective-permute-done((bf16[1024,512]{1,0:T(8,128)(2,1)S(1)}, bf16[1024,512]{1,0:T(8,128)(2,1)S(1)}, u32[]{:S(2)}, u32[]{:S(2)}) %collective-permute-start.1) | collective-permute-done | bytes 1048608 | tf_op jit(solution)/shard_map/cond/branch_0_fun/ppermute | solution.py:496
  54.2 0.0 all-to-all-done
  54.2 1.3 %collective-permute-start.2 = (bf16[1024,512]{1,0:T(8,128)(2,1)S(1)}, bf16[1024,512]{1,0:T(8,128)(2,1)S(1)}, u32[]{:S(2)}, u32[]{:S(2)}) collective-permute-start(bf16[1024,512]{1,0:T(8,128)(2,1)S(1)} %collective-permute-done.1.p3_ref), channel_id=1, source_target_pairs={{0,32},{224,192},{1,33},{225,193},{2,34},{226,194},{3,35},{227,195... | collective-permute-start | bytes 3145736 | tf_op jit(solution)/shard_map/cond/branch_0_fun/ppermute | solution.py:504
  55.5 3.4 %fetch.1 = bf16[512,8192]{1,0:T(8,128)(2,1)S(1)} custom-call(bf16[512,8192]{1,0:T(8,128)(2,1)} %get-tuple-element.12.w_hbm), custom_call_target="tpu_custom_call" | custom-call | flops 16777216 | bytes 16777216 | tf_op jit(solution)/shard_map/cond/branch_0_fun/fetch/pallas_call | solution.py:411
  58.9 0.0 collective-permute-done.2.p4_ref
  59.0 0.0 copy-done.1
  59.0 11.7 %crop_first.1 = (bf16[512,8192]{1,0:T(8,128)(2,1)S(1)}, f32[4,128]{1,0:T(4,128)S(1)}) custom-call(bf16[512,8192]{1,0:T(8,128)(2,1)} %get-tuple-element.12.w_hbm, s32[4,128]{1,0:T(4,128)S(1)} %copy-done.1, bf16[1024,512]{1,0:T(8,128)(2,1)S(1)} %stack_rows.1.both_ref, bf16[1024,512]{1,0:T(8,128)(2,1)S(1)} %collective-permute-done.1.p3_ref, ...), custom_call_target="tpu_custom_call" | custom-call | flops 4294967296 | bytes 16777216 | tf_op jit(solution)/shard_map/cond/branch_0_fun/crop_first/pallas_call | solution.py:411
  70.7 20.8 %all_to_all.29.cols_ref = bf16[8,8,1152]{2,1,0:T(8,128)(2,1)S(1)} all-to-all(bf16[8,8,1152]{2,1,0:T(8,128)(2,1)} %get-tuple-element.48), channel_id=1, replica_groups=mesh['sec'=8,'proto'=32] {'sec'}, dimensions={0} | all-to-all | bytes 294912 | tf_op jit(solution)/shard_map/all_to_all | solution.py:520
  91.5 0.0 copy-start
  91.5 6.9 %crop_product.1 = bf16[32,16,640]{2,1,0:T(8,128)(2,1)S(1)} custom-call(bf16[512,8192]{1,0:T(8,128)(2,1)S(1)} %get-tuple-element.47.ec_ref, bf16[8,8,1152]{2,1,0:T(8,128)(2,1)S(1)} %all_to_all.29.cols_ref, bf16[512,8192]{1,0:T(8,128)(2,1)S(1)} %get-tuple-element.49.w_ref, bf16[512,512]{1,0:T(8,128)(2,1)} %get-tuple-element.50.u_ref, s32[4,128]{1,0:T(4,128)} %bitcast.7, ...), custom_call_target="tpu_custom_call" | custom-call | flops 4294967296 | bytes 16777216 | tf_op jit(solution)/shard_map/crop_product/pallas_call | solution.py:411
  98.4 24.0 %all_to_all.30.c_ref = bf16[32,16,640]{2,1,0:T(8,128)(2,1)S(1)} all-to-all(bf16[32,16,640]{2,1,0:T(8,128)(2,1)S(1)} %crop_product.1), channel_id=1, replica_groups=mesh['sec'=8,'proto'=32] {'proto'}, dimensions={0} | all-to-all | bytes 1310720 | tf_op jit(solution)/shard_map/all_to_all | solution.py:454
  122.3 0.0 copy-done
  122.3 1.1 finish.1
  (2 shorter events, 0.0 us)
Async XLA Ops:
  0.6 0.7 collective-permute-start.5
  1.4 10.4 %slice-start = ((s8[8388608]{0:T(1024)(128)(4,1)}), s8[4194304]{0:T(1024)(128)(4,1)S(1)}, s32[]{:S(2)}) async-start(s8[8388608]{0:T(1024)(128)(4,1)} %bitcast.4), calls=%async_computation.6 | async-start | bytes 8388608 | tf_op jit(solution)/shard_map/cond
  1.4 10.4 %collective-permute-start = (bf16[512,512]{1,0:T(8,128)(2,1)S(1)}, bf16[512,512]{1,0:T(8,128)(2,1)S(1)}, u32[]{:S(2)}, u32[]{:S(2)}) collective-permute-start(bf16[512,512]{1,0:T(8,128)(2,1)S(1)} %get-tuple-element.14.p1_ref), channel_id=1, source_target_pairs={{64,160},{160,64},{65,161},{161,65},{66,162},{162,66},{67,163},{16... | collective-permute-start | bytes 1572872 | tf_op jit(solution)/shard_map/cond/branch_0_fun/ppermute | solution.py:492
  2.2 9.6 %slice-start.1 = ((s8[8388608]{0:T(1024)(128)(4,1)}), s8[4194304]{0:T(1024)(128)(4,1)S(1)}, s32[]{:S(2)}) async-start(s8[8388608]{0:T(1024)(128)(4,1)} %bitcast.4), calls=%async_computation.7 | async-start | bytes 8388608 | tf_op jit(solution)/shard_map/cond
  21.5 32.7 %all-to-all-start = ((bf16[32,16,640]{2,1,0:T(8,128)(2,1)}), bf16[32,16,640]{2,1,0:T(8,128)(2,1)S(1)}, u32[]{:S(2)}, u32[]{:S(2)}) async-start(bf16[32,16,640]{2,1,0:T(8,128)(2,1)} %student_product.1), calls=%async_computation | async-start | bytes 1310720 | tf_op jit(solution)/shard_map/cond/branch_0_fun/all_to_all | solution.py:454
  33.3 25.7 %copy-start.1 = (s32[4,128]{1,0:T(4,128)S(1)}, s32[4,128]{1,0:T(4,128)}, u32[]{:S(2)}) copy-start(s32[4,128]{1,0:T(4,128)} %get-tuple-element.13.index_ref) | copy-start | bytes 6148 | tf_op jit(solution)/shard_map/cond
  33.3 20.9 %collective-permute-start.1 = (bf16[1024,512]{1,0:T(8,128)(2,1)S(1)}, bf16[1024,512]{1,0:T(8,128)(2,1)S(1)}, u32[]{:S(2)}, u32[]{:S(2)}) collective-permute-start(bf16[1024,512]{1,0:T(8,128)(2,1)S(1)} %stack_rows.1.both_ref), channel_id=1, source_target_pairs={{64,0},{160,224},{65,1},{161,225},{66,2},{162,226},{67,3},{163,227... | collective-permute-start | bytes 3145736 | tf_op jit(solution)/shard_map/cond/branch_0_fun/ppermute | solution.py:496
  54.2 4.8 %collective-permute-start.2 = (bf16[1024,512]{1,0:T(8,128)(2,1)S(1)}, bf16[1024,512]{1,0:T(8,128)(2,1)S(1)}, u32[]{:S(2)}, u32[]{:S(2)}) collective-permute-start(bf16[1024,512]{1,0:T(8,128)(2,1)S(1)} %collective-permute-done.1.p3_ref), channel_id=1, source_target_pairs={{0,32},{224,192},{1,33},{225,193},{2,34},{226,194},{3,35},{227,195... | collective-permute-start | bytes 3145736 | tf_op jit(solution)/shard_map/cond/branch_0_fun/ppermute | solution.py:504
  91.5 30.9 %copy-start = (s32[512]{0:T(512)S(1)}, s32[512]{0:T(512)}, u32[]{:S(2)}) copy-start(s32[512]{0:T(512)} %param.9) | copy-start | bytes 6148

commit v2 on v1

--- a/solution.py
+++ b/solution.py
@@ -1,4 +1,5 @@
 import functools
+import math
 
 import jax
 import jax.numpy as jnp
@@ -11,6 +12,7 @@
 SAMPLES = 1024
 TEACH_TEMP = 0.07
 STUD_TEMP = 0.1
+TEACH_SCALE = math.log2(math.e) / TEACH_TEMP
 
 F32 = jnp.float32
 BF16 = jnp.bfloat16
@@ -145,8 +147,11 @@
     lax.fori_loop(0, rows // block, step, 0)
 
 
-def first_logits(x_ref, w_hbm, l_ref, u_ref, send_ref, top_ref, w_ref, sems, *, scale):
+def first_logits(x_hbm, w_hbm, l_ref, send_ref, u_ref, x_ref, top_ref, w_ref, x_sem, sems, *, scale):
+    copy = pltpu.make_async_copy(x_hbm, x_ref, x_sem)
+    copy.start()
     start_stream(w_hbm, w_ref, sems)
+    copy.wait()
     u_ref[...] = unit_rows(x_ref[...])
 
     def wait(j):
@@ -169,7 +174,7 @@
 
         def inner(i, acc):
             r = pl.ds(pl.multiple_of(i * block, block), block)
-            x = jnp.exp(l_ref[r, at] - tile_lanes(top_ref[r, :], width // LANES))
+            x = jnp.exp2(l_ref[r, at] - tile_lanes(top_ref[r, :], width // LANES))
             e_ref[r, at] = x
             return acc + jnp.sum(x.reshape(block // SUBS, SUBS, width), axis=0)
 
@@ -285,7 +290,7 @@
         wait_stream(w_hbm, w_ref, sems, j)
 
     chunk = w_ref.shape[1] // sems.shape[0]
-    logits_into(crop_ref, w_ref, lc_ref, top_ref, 1.0 / TEACH_TEMP, wait, chunk)
+    logits_into(crop_ref, w_ref, lc_ref, top_ref, TEACH_SCALE, wait, chunk)
     row = lanes_to_row(top_ref[...], jnp.max)
     send_ref[...] = pack_row(row)
     top_ref[...] = row_to_column(row)
@@ -296,7 +301,7 @@
 
         def inner(i, carry):
             r = pl.ds(pl.multiple_of(i * block, block), block)
-            x = jnp.exp(lc_ref[r, at] - tile_lanes(top_ref[r, :], width // LANES))
+            x = jnp.exp2(lc_ref[r, at] - tile_lanes(top_ref[r, :], width // LANES))
             ec_ref[r, at] = x.astype(BF16)
             return carry
 
@@ -324,16 +329,16 @@
             tops = owner[t : t + 1, size:]
             picked = jnp.where(index == lane + (s * rows + t * LANES), tops, picked)
     picked = jnp.sum(picked, axis=1, keepdims=True)
-    fix_ref[...] = jnp.exp(row_to_column(unpack_row(top_ref[...])) - picked)
+    fix_ref[...] = jnp.exp2(row_to_column(unpack_row(top_ref[...])) - picked)
     c_ref[...] = jnp.zeros_like(c_ref)
     acc_ref[...] = jnp.zeros_like(acc_ref)
 
     def step(j, carry):
         at = pl.ds(pl.multiple_of(j * chunk, chunk), chunk)
-        y = ec_ref[:, at].astype(F32) * scale_ref[:, at]
-        acc_ref[...] += fold_lanes(jnp.add, y)
+        y = (ec_ref[:, at].astype(F32) * scale_ref[:, at]).astype(BF16)
+        acc_ref[...] += fold_lanes(jnp.add, y.astype(F32))
         c_ref[...] += lax.dot_general(
-            y.astype(BF16), w_ref[:, at], (((1,), (1,)), ((), ())), preferred_element_type=F32
+            y, w_ref[:, at], (((1,), (1,)), ((), ())), preferred_element_type=F32
         )
         return carry
 
@@ -345,7 +350,32 @@
     write_parts(send_ref, c_ref[...], [*total, *cross])
 
 
-def finish(a_ref, c_ref, live_ref, grad_ref, loss_ref, weight_ref, stud_ref, targ_ref):
+def student_finish(a_ref, live_ref, stud_ref, log_ref, weight_ref, scale_ref):
+    each, width = stud_ref.shape
+    packs = live_ref.shape[0]
+    parts = a_ref.shape[0]
+    extra = a_ref[:, :, width:].astype(F32)
+    tops = extra[:, :packs]
+    top = jnp.max(tops, axis=0)
+    weight = jnp.exp(tops - top[None])
+    sums = extra[:, packs : 2 * packs] + extra[:, 2 * packs : 3 * packs]
+    total = jnp.sum(weight * sums, axis=0)
+    log_ref[...] = top + jnp.log(total)
+    rest = jnp.zeros((LANES - parts, LANES), F32)
+    for i in range(packs):
+        piece = jnp.concatenate([weight[:, i, :], rest], axis=0)
+        weight_ref[i * LANES : (i + 1) * LANES, :] = jnp.transpose(piece)
+    scale = live_ref[...].astype(F32) * (1.0 / STUD_TEMP) / total
+    scale_ref[...] = row_to_column(unpack_row(scale))
+    mine = pl.ds(pl.multiple_of(lax.axis_index("proto") * each, each), each)
+    factor = weight_ref[mine, :]
+    stud = jnp.zeros(stud_ref.shape, F32)
+    for p in range(parts):
+        stud += a_ref[p, :, :width].astype(F32) * factor[:, p : p + 1]
+    stud_ref[...] = stud * tile_lanes(scale_ref[mine, :], width // LANES)
+
+
+def finish(stud_ref, log_ref, c_ref, live_ref, grad_ref, loss_ref, scale_ref):
     each, width = grad_ref.shape
     packs = live_ref.shape[0]
     teacher = is_teacher()
@@ -357,35 +387,15 @@
 
     @pl.when(jnp.logical_not(teacher))
     def _():
-        parts = a_ref.shape[0]
-        extra = a_ref[:, :, width:].astype(F32)
-        tops = extra[:, :packs]
-        top = jnp.max(tops, axis=0)
-        weight = jnp.exp(tops - top[None])
-        sums = extra[:, packs : 2 * packs] + extra[:, 2 * packs : 3 * packs]
-        total = jnp.sum(weight * sums, axis=0)
-        rest = jnp.zeros((LANES - parts, LANES), F32)
-        for i in range(packs):
-            piece = jnp.concatenate([weight[:, i, :], rest], axis=0)
-            weight_ref[i * LANES : (i + 1) * LANES, :] = jnp.transpose(piece)
         extra = jnp.sum(c_ref[:, :, width:].astype(F32), axis=0)
         target_sum = extra[:packs] + extra[packs : 2 * packs]
         cross = extra[2 * packs : 3 * packs] + extra[3 * packs :]
         live = live_ref[...].astype(F32)
-        loss_ref[...] = live * (top + jnp.log(total) - cross / target_sum)
-        scale = live * (1.0 / STUD_TEMP)
-        stud_ref[...] = row_to_column(unpack_row(scale / total))
-        targ_ref[...] = row_to_column(unpack_row(scale / target_sum))
+        loss_ref[...] = live * (log_ref[...] - cross / target_sum)
+        scale_ref[...] = row_to_column(unpack_row(live * (1.0 / STUD_TEMP) / target_sum))
         mine = pl.ds(pl.multiple_of(lax.axis_index("proto") * each, each), each)
-        tiles = width // LANES
-        factor = weight_ref[mine, :]
-        stud = jnp.zeros(grad_ref.shape, F32)
-        for p in range(parts):
-            stud += a_ref[p, :, :width].astype(F32) * factor[:, p : p + 1]
         targ = jnp.sum(c_ref[:, :, :width].astype(F32), axis=0)
-        grad_ref[...] = stud * tile_lanes(stud_ref[mine, :], tiles) - targ * tile_lanes(
-            targ_ref[mine, :], tiles
-        )
+        grad_ref[...] = stud_ref[...] - targ * tile_lanes(scale_ref[mine, :], width // LANES)
 
 
 def fetch(w_hbm, w_ref, sem):
@@ -431,6 +441,7 @@
     row_send = ((protos, packs, LANES), F32)
     one_row = ((packs, LANES), F32)
     parts = ((protos, each, width + LANES), BF16)
+    part_rows = ((each, width), F32)
     column = ((1, cols), F32)
     columns = ((secs, 8, cols // 8 + LANES), BF16)
     table = ((rows, cols), F32)
@@ -456,17 +467,21 @@
     def unused(after, *out):
         return call(hollow, out, [after], spaces=[pl.ANY], out_space=pl.ANY)
 
-    def start(temp, send):
+    def start(scale, send, keep):
+        unit = VMEM(*units)
         return call(
-            functools.partial(first_logits, scale=1.0 / temp),
-            [table, units, send],
+            functools.partial(first_logits, scale=scale),
+            [table, send, units] if keep else [table, send],
             [features, prototypes],
-            [lanes, protos_vmem, sems(4)],
-            flops=gemm, moved=big, spaces=[VMEM, HBM], limit=32, name="first_logits",
+            [
+                *([] if keep else [unit]), unit, lanes, protos_vmem,
+                pltpu.SemaphoreType.DMA, sems(4),
+            ],
+            flops=gemm, moved=big, spaces=[HBM, HBM], limit=32, name="first_logits",
         )
 
     def teacher(p1):
-        logits, _, send = start(TEACH_TEMP, row_send)
+        logits, send = start(TEACH_SCALE, row_send, False)
         top_got = spread(send)
         expo, col = call(
             teacher_exponentials, [table, column], [logits, top_got], [lanes], {0: 0},
@@ -486,11 +501,13 @@
                 (col,) = call(
                     teacher_columns, [column], [expo, got], [lanes], flops=big, moved=big
                 )
-        return col, *unused(col, crop_table, crop_table, units, one_row, parts)
+        return col, *unused(
+            col, crop_table, crop_table, units, one_row, part_rows, one_row
+        )
 
     def student(p1):
         p2 = lax.ppermute(p1, "sec", [(2, 5), (5, 2)])
-        logits, unit, top = start(STUD_TEMP, one_row)
+        logits, top, unit = start(1.0 / STUD_TEMP, one_row, True)
         top, p2 = lax.optimization_barrier((top, p2))
         (both,) = call(stack_rows, [both_rows], [p1, p2])
         p3 = lax.ppermute(both, "sec", [(2, 0), (5, 7)])
@@ -513,10 +530,15 @@
             fetch, [crop_table], [prototypes], [pltpu.SemaphoreType.DMA],
             flops=big, moved=big, spaces=[HBM],
         )
-        return *unused(crop_expo, columns), crop_expo, protos_here, unit, crop_top, stud_got
+        stud, log_total = call(
+            student_finish, [part_rows, one_row], [stud_got, live], [lanes, lanes]
+        )
+        return *unused(crop_expo, columns), crop_expo, protos_here, unit, crop_top, stud, log_total
 
     p1 = lax.ppermute(features, "sec", [(3, 2), (4, 5)])
-    col, expo, protos_here, unit, crop_top, stud_got = lax.cond(is_teacher(), teacher, student, p1)
+    col, expo, protos_here, unit, crop_top, stud, log_total = lax.cond(
+        is_teacher(), teacher, student, p1
+    )
     cols_got = lax.all_to_all(col, "sec", 0, 0, tiled=True)
     (send,) = call(
         crop_product,
@@ -527,9 +549,9 @@
     )
     grad, loss = call(
         finish,
-        [((each, width), F32), ((packs, LANES), F32)],
-        [stud_got, spread(send), live],
-        [lanes, lanes, lanes],
+        [part_rows, one_row],
+        [stud, log_total, spread(send), live],
+        [lanes],
     )
     return loss.reshape(rows), grad
 

time: 124 us -> 123 us (level)
    pallas_call x8 -> x9, Pallas kernels: 42.5 us -> 41.5 us  [call(): pl.pallas_call(kernel, name=name or kernel.__name__, out_shape=tuple((jax...]
  transfers between devices with their start and end apart: 5 -> 5, of which waited for: 1 -> 1; matrix products, arithmetic and copies ran while one was open for 0% -> 0% of each run, Pallas kernels for 11% -> 10%
where the time goes in v2:
time: 123 us; the launch traced here: 122 us
  blocking collectives  44.3 us (36%)
  Pallas kernels  41.5 us (34%)
  waiting for transfers between devices  19.6 us (16%)
  starting transfers between devices  15.8 us (13%)
    pallas_call x9, Pallas kernels, call(): pl.pallas_call(kernel, name=name or kernel.__name__, out_shape=tuple((jax...  41.5 us
    all_to_all x1, blocking collectives, spread(): return lax.all_to_all(x, 'proto', 0, 0, tiled=True)  23.9 us
    all_to_all x1, blocking collectives, per_device(): cols_got = lax.all_to_all(col, 'sec', 0, 0, tiled=True)  20.3 us
    ppermute x1, waiting for transfers between devices, student(): p3 = lax.ppermute(both, 'sec', [(2, 0), (5, 7)])  19.6 us
    all_to_all x1, starting transfers between devices, spread(): return lax.all_to_all(x, 'proto', 0, 0, tiled=True)  11.6 us
  transfers between devices with their start and end apart: 5, of which 1 were waited for; matrix products, arithmetic and copies ran while one was open for 0% of the time, Pallas kernels for 10%

profile of v2, /device:TPU:2, one launch (start us, length us, event | category | flops | bytes accessed | tf_op | source)
XLA Modules:
  0.0 122.0 jit_solution(2547342910595968886)
XLA Ops:
  0.6 0.7 collective-permute-start.5
  1.3 0.0 collective-permute-done.5
  1.4 68.7 %conditional.1 = (bf16[8,8,1152]{2,1,0:T(8,128)(2,1)}, bf16[512,8192]{1,0:T(8,128)(2,1)S(1)}, bf16[512,8192]{1,0:T(8,128)(2,1)S(1)}, bf16[512,512]{1,0:T(8,128)(...) conditional(s32[]{:T(128)} %convert_element_type.3, (bf16[512,512]{1,0:T(8,128)(2,1)}, ...), branch_computations={%region_0.0_spmd, %region_1.0_spmd} | conditional | flops 12901679104 | bytes 104743216 | solution.py:539
  1.4 0.0 slice-start
  1.4 0.8 collective-permute-start
  2.2 0.0 slice-start.1
  2.2 8.6 %first_logits.2 = (f32[512,8192]{1,0:T(8,128)S(1)}, f32[4,128]{1,0:T(4,128)S(1)}, bf16[512,512]{1,0:T(8,128)(2,1)}) custom-call(bf16[512,512]{1,0:T(8,128)(2,1)} %get-tuple-element.17.x_hbm, bf16[512,8192]{1,0:T(8,128)(2,1)} %get-tuple-element.14.w_hbm), custom_call_target="tpu_custom_call" | custom-call | flops 4294967296 | bytes 16777216 | tf_op jit(solution)/shard_map/cond/branch_0_fun/first_logits/pallas_call | solution.py:421
  10.8 0.0 collective-permute-done.p2_ref
  10.8 0.0 slice-done
  10.9 0.0 slice-done.1
  10.9 9.7 %student_product.1 = bf16[32,16,640]{2,1,0:T(8,128)(2,1)} custom-call(f32[512,8192]{1,0:T(8,128)S(1)} %get-tuple-element.20.l_ref, f32[4,128]{1,0:T(4,128)S(1)} %get-tuple-element.21.top_ref, bf16[512,8192]{1,0:T(8,128)(2,1)S(1)} %bitcast.4), custom_call_target="tpu_custom_call" | custom-call | flops 4294967296 | bytes 16777216 | tf_op jit(solution)/shard_map/cond/branch_0_fun/student_product/pallas_call | solution.py:421
  20.6 11.6 %all-to-all-start = ((bf16[32,16,640]{2,1,0:T(8,128)(2,1)}), bf16[32,16,640]{2,1,0:T(8,128)(2,1)S(1)}, u32[]{:S(2)}, u32[]{:S(2)}) async-start(bf16[32,16,640]{2,1,0:T(8,128)(2,1)} %student_product.1), calls=%async_computation | async-start | bytes 1310720 | tf_op jit(solution)/shard_map/cond/branch_0_fun/all_to_all | solution.py:465
  32.2 0.1 stack_rows.1.both_ref
  32.3 0.0 copy-start.1
  32.3 0.0 copy-start.2
  32.3 1.3 %collective-permute-start.1 = (bf16[1024,512]{1,0:T(8,128)(2,1)S(1)}, bf16[1024,512]{1,0:T(8,128)(2,1)S(1)}, u32[]{:S(2)}, u32[]{:S(2)}) collective-permute-start(bf16[1024,512]{1,0:T(8,128)(2,1)S(1)} %stack_rows.1.both_ref), channel_id=1, source_target_pairs={{64,0},{160,224},{65,1},{161,225},{66,2},{162,226},{67,3},{163,227... | collective-permute-start | bytes 3145736 | tf_op jit(solution)/shard_map/cond/branch_0_fun/ppermute | solution.py:513
  33.6 19.6 %collective-permute-done.1.p3_ref = bf16[1024,512]{1,0:T(8,128)(2,1)S(1)} collective-permute-done((bf16[1024,512]{1,0:T(8,128)(2,1)S(1)}, bf16[1024,512]{1,0:T(8,128)(2,1)S(1)}, u32[]{:S(2)}, u32[]{:S(2)}) %collective-permute-start.1) | collective-permute-done | bytes 1048608 | tf_op jit(solution)/shard_map/cond/branch_0_fun/ppermute | solution.py:513
  53.2 0.0 all-to-all-done.a_ref
  53.2 1.3 %collective-permute-start.2 = (bf16[1024,512]{1,0:T(8,128)(2,1)S(1)}, bf16[1024,512]{1,0:T(8,128)(2,1)S(1)}, u32[]{:S(2)}, u32[]{:S(2)}) collective-permute-start(bf16[1024,512]{1,0:T(8,128)(2,1)S(1)} %collective-permute-done.1.p3_ref), channel_id=1, source_target_pairs={{0,32},{224,192},{1,33},{225,193},{2,34},{226,194},{3,35},{227,195... | collective-permute-start | bytes 3145736 | tf_op jit(solution)/shard_map/cond/branch_0_fun/ppermute | solution.py:521
  54.6 3.4 %fetch.1 = bf16[512,8192]{1,0:T(8,128)(2,1)S(1)} custom-call(bf16[512,8192]{1,0:T(8,128)(2,1)} %get-tuple-element.14.w_hbm), custom_call_target="tpu_custom_call" | custom-call | flops 16777216 | bytes 16777216 | tf_op jit(solution)/shard_map/cond/branch_0_fun/fetch/pallas_call | solution.py:421
  58.0 0.0 copy-done.1
  58.0 0.4 student_finish.1
  58.4 0.0 collective-permute-done.2.p4_ref
  58.4 0.0 copy-done.2
  58.4 11.6 %crop_first.1 = (bf16[512,8192]{1,0:T(8,128)(2,1)S(1)}, f32[4,128]{1,0:T(4,128)S(1)}) custom-call(bf16[512,8192]{1,0:T(8,128)(2,1)} %get-tuple-element.14.w_hbm, s32[4,128]{1,0:T(4,128)S(1)} %copy-done.2, bf16[1024,512]{1,0:T(8,128)(2,1)S(1)} %stack_rows.1.both_ref, bf16[1024,512]{1,0:T(8,128)(2,1)S(1)} %collective-permute-done.1.p3_ref, ...), custom_call_target="tpu_custom_call" | custom-call | flops 4294967296 | bytes 16777216 | tf_op jit(solution)/shard_map/cond/branch_0_fun/crop_first/pallas_call | solution.py:421
  70.1 20.3 %all_to_all.29.cols_ref = bf16[8,8,1152]{2,1,0:T(8,128)(2,1)S(1)} all-to-all(bf16[8,8,1152]{2,1,0:T(8,128)(2,1)} %get-tuple-element.56), channel_id=1, replica_groups=mesh['sec'=8,'proto'=32] {'sec'}, dimensions={0} | all-to-all | bytes 294912 | tf_op jit(solution)/shard_map/all_to_all | solution.py:542
  90.4 0.0 copy-start
  90.4 6.9 %crop_product.1 = bf16[32,16,640]{2,1,0:T(8,128)(2,1)S(1)} custom-call(bf16[512,8192]{1,0:T(8,128)(2,1)S(1)} %get-tuple-element.55.ec_ref, bf16[8,8,1152]{2,1,0:T(8,128)(2,1)S(1)} %all_to_all.29.cols_ref, bf16[512,8192]{1,0:T(8,128)(2,1)S(1)} %get-tuple-element.57.w_ref, bf16[512,512]{1,0:T(8,128)(2,1)} %get-tuple-element.58.u_ref, s32[4,128]{1,0:T(4,128)} %bitcast.8, ...), custom_call_target="tpu_custom_call" | custom-call | flops 4294967296 | bytes 16777216 | tf_op jit(solution)/shard_map/crop_product/pallas_call | solution.py:421
  97.3 23.9 %all_to_all.30.c_ref = bf16[32,16,640]{2,1,0:T(8,128)(2,1)S(1)} all-to-all(bf16[32,16,640]{2,1,0:T(8,128)(2,1)S(1)} %crop_product.1), channel_id=1, replica_groups=mesh['sec'=8,'proto'=32] {'proto'}, dimensions={0} | all-to-all | bytes 1310720 | tf_op jit(solution)/shard_map/all_to_all | solution.py:465
  121.2 0.0 copy-done
  121.2 0.8 finish.1
  (2 shorter events, 0.0 us)
Async XLA Ops:
  0.6 0.7 collective-permute-start.5
  1.4 9.5 %slice-start = ((s8[8388608]{0:T(1024)(128)(4,1)}), s8[4194304]{0:T(1024)(128)(4,1)S(1)}, s32[]{:S(2)}) async-start(s8[8388608]{0:T(1024)(128)(4,1)} %bitcast.3), calls=%async_computation.6 | async-start | bytes 8388608 | tf_op jit(solution)/shard_map/cond
  1.4 9.5 %collective-permute-start = (bf16[512,512]{1,0:T(8,128)(2,1)S(1)}, bf16[512,512]{1,0:T(8,128)(2,1)S(1)}, u32[]{:S(2)}, u32[]{:S(2)}) collective-permute-start(bf16[512,512]{1,0:T(8,128)(2,1)S(1)} %get-tuple-element.16.p1_ref), channel_id=1, source_target_pairs={{64,160},{160,64},{65,161},{161,65},{66,162},{162,66},{67,163},{16... | collective-permute-start | bytes 1572872 | tf_op jit(solution)/shard_map/cond/branch_0_fun/ppermute | solution.py:509
  2.2 8.7 %slice-start.1 = ((s8[8388608]{0:T(1024)(128)(4,1)}), s8[4194304]{0:T(1024)(128)(4,1)S(1)}, s32[]{:S(2)}) async-start(s8[8388608]{0:T(1024)(128)(4,1)} %bitcast.3), calls=%async_computation.7 | async-start | bytes 8388608 | tf_op jit(solution)/shard_map/cond
  20.6 32.7 %all-to-all-start = ((bf16[32,16,640]{2,1,0:T(8,128)(2,1)}), bf16[32,16,640]{2,1,0:T(8,128)(2,1)S(1)}, u32[]{:S(2)}, u32[]{:S(2)}) async-start(bf16[32,16,640]{2,1,0:T(8,128)(2,1)} %student_product.1), calls=%async_computation | async-start | bytes 1310720 | tf_op jit(solution)/shard_map/cond/branch_0_fun/all_to_all | solution.py:465
  32.3 25.7 %copy-start.1 = (s32[4,128]{1,0:T(4,128)S(1)}, s32[4,128]{1,0:T(4,128)}, u32[]{:S(2)}) copy-start(s32[4,128]{1,0:T(4,128)} %get-tuple-element.27.live_ref) | copy-start | bytes 6148 | tf_op jit(solution)/shard_map/cond
  32.3 26.1 %copy-start.2 = (s32[4,128]{1,0:T(4,128)S(1)}, s32[4,128]{1,0:T(4,128)}, u32[]{:S(2)}) copy-start(s32[4,128]{1,0:T(4,128)} %get-tuple-element.15.index_ref) | copy-start | bytes 6148 | tf_op jit(solution)/shard_map/cond
  32.3 20.9 %collective-permute-start.1 = (bf16[1024,512]{1,0:T(8,128)(2,1)S(1)}, bf16[1024,512]{1,0:T(8,128)(2,1)S(1)}, u32[]{:S(2)}, u32[]{:S(2)}) collective-permute-start(bf16[1024,512]{1,0:T(8,128)(2,1)S(1)} %stack_rows.1.both_ref), channel_id=1, source_target_pairs={{64,0},{160,224},{65,1},{161,225},{66,2},{162,226},{67,3},{163,227... | collective-permute-start | bytes 3145736 | tf_op jit(solution)/shard_map/cond/branch_0_fun/ppermute | solution.py:513
  53.2 5.2 %collective-permute-start.2 = (bf16[1024,512]{1,0:T(8,128)(2,1)S(1)}, bf16[1024,512]{1,0:T(8,128)(2,1)S(1)}, u32[]{:S(2)}, u32[]{:S(2)}) collective-permute-start(bf16[1024,512]{1,0:T(8,128)(2,1)S(1)} %collective-permute-done.1.p3_ref), channel_id=1, source_target_pairs={{0,32},{224,192},{1,33},{225,193},{2,34},{226,194},{3,35},{227,195... | collective-permute-start | bytes 3145736 | tf_op jit(solution)/shard_map/cond/branch_0_fun/ppermute | solution.py:521
  90.4 30.9 %copy-start = (s32[512]{0:T(512)S(1)}, s32[512]{0:T(512)}, u32[]{:S(2)}) copy-start(s32[512]{0:T(512)} %param.9) | copy-start | bytes 6148

commit v3 on v2

--- a/solution.py
+++ b/solution.py
@@ -8,6 +8,7 @@
 from jax.experimental.pallas import tpu as pltpu
 from jax.sharding import PartitionSpec as P
 
+
 PROTOS = 262144
 SAMPLES = 1024
 TEACH_TEMP = 0.07
@@ -21,6 +22,7 @@
 
 TEACH_A = 3
 TEACH_B = 4
+
 
 def is_teacher():
     sec = lax.axis_index("sec")
@@ -242,6 +244,18 @@
     lax.fori_loop(0, sems.shape[0], step, 0)
     high, low = split_high(pack_row(lanes_to_row(sum_ref[...], jnp.sum)))
     write_parts(send_ref, acc_ref[...], [packed, high, low, jnp.zeros_like(low)])
+
+
+def pick_rows(p1_ref, p0_ref, rows_ref):
+    near = lax.axis_index("proto") < lax.axis_size("proto") // 2
+
+    @pl.when(near)
+    def _():
+        rows_ref[...] = p1_ref[...]
+
+    @pl.when(jnp.logical_not(near))
+    def _():
+        rows_ref[...] = p0_ref[...]
 
 
 def stack_rows(p1_ref, p2_ref, both_ref):
@@ -414,13 +428,12 @@
 
 
 def call(
-    kernel, out, args, scratch=(), alias=None, flops=0, moved=0, limit=8, spaces=None, name=None,
+    kernel, out, args, scratch=(), alias=None, flops=0, moved=0, limit=8, spaces=None,
     out_space=VMEM,
 ):
     spaces = spaces or [VMEM] * len(args)
     return pl.pallas_call(
         kernel,
-        name=name or kernel.__name__,
         out_shape=tuple(jax.ShapeDtypeStruct(s, d) for s, d in out),
         in_specs=[pl.BlockSpec(memory_space=s) for s in spaces],
         out_specs=tuple([pl.BlockSpec(memory_space=out_space)] * len(out)),
@@ -477,7 +490,7 @@
                 *([] if keep else [unit]), unit, lanes, protos_vmem,
                 pltpu.SemaphoreType.DMA, sems(4),
             ],
-            flops=gemm, moved=big, spaces=[HBM, HBM], limit=32, name="first_logits",
+            flops=gemm, moved=big, spaces=[HBM, HBM], limit=32,
         )
 
     def teacher(p1):
@@ -506,10 +519,14 @@
         )
 
     def student(p1):
-        p2 = lax.ppermute(p1, "sec", [(2, 5), (5, 2)])
+        across = [(s * protos + p, s * protos + p + half) for s in (2, 5) for p in range(half)]
+        p0 = lax.ppermute(p1, ("sec", "proto"), across)
         logits, top, unit = start(1.0 / STUD_TEMP, one_row, True)
-        top, p2 = lax.optimization_barrier((top, p2))
-        (both,) = call(stack_rows, [both_rows], [p1, p2])
+        top, p0 = lax.optimization_barrier((top, p0))
+        (rows_here,) = call(pick_rows, [units], [p1, p0])
+        p2 = lax.ppermute(rows_here, "sec", [(2, 5), (5, 2)])
+        (both,) = call(stack_rows, [both_rows], [rows_here, p2])
+        top, both = lax.optimization_barrier((top, both))
         p3 = lax.ppermute(both, "sec", [(2, 0), (5, 7)])
         (send,) = call(
             student_product, [parts], [logits, top, prototypes],
@@ -535,7 +552,10 @@
         )
         return *unused(crop_expo, columns), crop_expo, protos_here, unit, crop_top, stud, log_total
 
-    p1 = lax.ppermute(features, "sec", [(3, 2), (4, 5)])
+    half = protos // 2
+    moves = [(3 * protos + p, 2 * protos + p) for p in range(half)]
+    moves += [(4 * protos + p, 5 * protos + p) for p in range(half)]
+    p1 = lax.ppermute(features, ("sec", "proto"), moves)
     col, expo, protos_here, unit, crop_top, stud, log_total = lax.cond(
         is_teacher(), teacher, student, p1
     )

time: 123 us -> 134 us (1.089)
  waiting for transfers between devices: 19.6 us -> 35.5 us
  blocking collectives: 44.3 us -> 38.6 us
    ppermute x1, waiting for transfers between devices: 19.6 us -> 35.5 us  [student(): p3 = lax.ppermute(both, 'sec', [(2, 0), (5, 7)])]
    all_to_all x1, blocking collectives: 20.3 us -> 9.57 us  [per_device(): cols_got = lax.all_to_all(col, 'sec', 0, 0, tiled=True)]
    all_to_all x1, blocking collectives: 23.9 us -> 29 us  [spread(): return lax.all_to_all(x, 'proto', 0, 0, tiled=True)]
    pallas_call x9 -> x10, Pallas kernels: 41.5 us -> 41.8 us  [call(): pl.pallas_call(kernel, out_shape=tuple((jax.ShapeDtypeStruct(s, d) for s,...]
  transfers between devices with their start and end apart: 5 -> 6, of which waited for: 1 -> 1; matrix products, arithmetic and copies ran while one was open for 0% -> 0% of each run, Pallas kernels for 10% -> 10%
where the time goes in v3:
time: 134 us; the launch traced here: 133 us
  Pallas kernels  41.8 us (31%)
  blocking collectives  38.6 us (29%)
  waiting for transfers between devices  35.5 us (26%)
  starting transfers between devices  16.4 us (12%)
    pallas_call x10, Pallas kernels, call(): pl.pallas_call(kernel, out_shape=tuple((jax.ShapeDtypeStruct(s, d) for s,...  41.8 us
    ppermute x1, waiting for transfers between devices, student(): p3 = lax.ppermute(both, 'sec', [(2, 0), (5, 7)])  35.5 us
    all_to_all x1, blocking collectives, spread(): return lax.all_to_all(x, 'proto', 0, 0, tiled=True)  29 us
    all_to_all x1, starting transfers between devices, spread(): return lax.all_to_all(x, 'proto', 0, 0, tiled=True)  11.6 us
    all_to_all x1, blocking collectives, per_device(): cols_got = lax.all_to_all(col, 'sec', 0, 0, tiled=True)  9.57 us
  transfers between devices with their start and end apart: 6, of which 1 were waited for; matrix products, arithmetic and copies ran while one was open for 0% of the time, Pallas kernels for 10%

profile of v3, /device:TPU:2, one launch (start us, length us, event | category | flops | bytes accessed | tf_op | source)
XLA Modules:
  0.0 133.2 jit_solution(9432593658882232264)
XLA Ops:
  0.6 0.7 collective-permute-start.6
  1.3 0.0 collective-permute-done.6
  1.4 85.5 %conditional.1 = (bf16[8,8,1152]{2,1,0:T(8,128)(2,1)}, bf16[512,8192]{1,0:T(8,128)(2,1)S(1)}, bf16[512,8192]{1,0:T(8,128)(2,1)S(1)}, bf16[512,512]{1,0:T(8,128)(...) conditional(s32[]{:T(128)} %convert_element_type.3, (bf16[512,512]{1,0:T(8,128)(2,1)}, ...), branch_computations={%region_0.0_spmd, %region_1.0_spmd} | conditional | flops 12901679104 | bytes 106840416 | solution.py:559
  1.4 0.7 collective-permute-start
  2.1 0.0 slice-start
  2.1 0.0 slice-start.1
  2.1 8.9 %branch_0_fun.8 = (f32[512,8192]{1,0:T(8,128)S(1)}, f32[4,128]{1,0:T(4,128)S(1)}, bf16[512,512]{1,0:T(8,128)(2,1)}) custom-call(bf16[512,512]{1,0:T(8,128)(2,1)} %get-tuple-element.16.x_hbm, bf16[512,8192]{1,0:T(8,128)(2,1)} %get-tuple-element.14.w_hbm), custom_call_target="tpu_custom_call" | custom-call | flops 4294967296 | bytes 16777216 | tf_op jit(solution)/shard_map/cond/branch_0_fun/pallas_call | solution.py:435
  11.0 0.0 collective-permute-done.p0_ref
  11.1 0.7 collective-permute-start.1
  11.8 0.0 collective-permute-done.1.p2_ref
  11.8 0.1 branch_0_fun.10.both_ref
  11.9 0.0 slice-done
  11.9 0.0 slice-done.1
  11.9 9.7 %branch_0_fun.11 = bf16[32,16,640]{2,1,0:T(8,128)(2,1)} custom-call(f32[512,8192]{1,0:T(8,128)S(1)} %get-tuple-element.22.l_ref, f32[4,128]{1,0:T(4,128)S(1)} %get-tuple-element.23.top_ref, bf16[512,8192]{1,0:T(8,128)(2,1)S(1)} %bitcast.4), custom_call_target="tpu_custom_call" | custom-call | flops 4294967296 | bytes 16777216 | tf_op jit(solution)/shard_map/cond/branch_0_fun/pallas_call | solution.py:435
  21.6 11.6 %all-to-all-start = ((bf16[32,16,640]{2,1,0:T(8,128)(2,1)}), bf16[32,16,640]{2,1,0:T(8,128)(2,1)S(1)}, u32[]{:S(2)}, u32[]{:S(2)}) async-start(bf16[32,16,640]{2,1,0:T(8,128)(2,1)} %branch_0_fun.11), calls=%async_computation | async-start | bytes 1310720 | tf_op jit(solution)/shard_map/cond/branch_0_fun/all_to_all | solution.py:478
  33.2 0.0 copy-start.1
  33.2 0.0 copy-start.2
  33.2 1.3 collective-permute-start.2
  34.5 35.5 %collective-permute-done.2.p3_ref = bf16[1024,512]{1,0:T(8,128)(2,1)S(1)} collective-permute-done((bf16[1024,512]{1,0:T(8,128)(2,1)S(1)}, bf16[1024,512]{1,0:T(8,128)(2,1)S(1)}, u32[]{:S(2)}, u32[]{:S(2)}) %collective-permute-start.2) | collective-permute-done | bytes 1048608 | tf_op jit(solution)/shard_map/cond/branch_0_fun/ppermute | solution.py:530
  70.0 0.0 all-to-all-done.a_ref
  70.0 1.3 %collective-permute-start.3 = (bf16[1024,512]{1,0:T(8,128)(2,1)S(1)}, bf16[1024,512]{1,0:T(8,128)(2,1)S(1)}, u32[]{:S(2)}, u32[]{:S(2)}) collective-permute-start(bf16[1024,512]{1,0:T(8,128)(2,1)S(1)} %collective-permute-done.2.p3_ref), channel_id=1, source_target_pairs={{0,32},{224,192},{1,33},{225,193},{2,34},{226,194},{3,35},{227,195... | collective-permute-start | bytes 3145736 | tf_op jit(solution)/shard_map/cond/branch_0_fun/ppermute | solution.py:538
  71.4 3.4 %branch_0_fun.14 = bf16[512,8192]{1,0:T(8,128)(2,1)S(1)} custom-call(bf16[512,8192]{1,0:T(8,128)(2,1)} %get-tuple-element.14.w_hbm), custom_call_target="tpu_custom_call" | custom-call | flops 16777216 | bytes 16777216 | tf_op jit(solution)/shard_map/cond/branch_0_fun/pallas_call | solution.py:435
  74.8 0.0 copy-done.1
  74.8 0.4 branch_0_fun.15
  75.2 0.0 collective-permute-done.3.p4_ref
  75.2 0.0 copy-done.2
  75.2 11.6 %branch_0_fun.12 = (bf16[512,8192]{1,0:T(8,128)(2,1)S(1)}, f32[4,128]{1,0:T(4,128)S(1)}) custom-call(bf16[512,8192]{1,0:T(8,128)(2,1)} %get-tuple-element.14.w_hbm, s32[4,128]{1,0:T(4,128)S(1)} %copy-done.2, bf16[1024,512]{1,0:T(8,128)(2,1)S(1)} %branch_0_fun.10.both_ref, bf16[1024,512]{1,0:T(8,128)(2,1)S(1)} %collective-permute-done.2.p3_ref, ...), custom_call_target="tpu_custom_call" | custom-call | flops 4294967296 | bytes 16777216 | tf_op jit(solution)/shard_map/cond/branch_0_fun/pallas_call | solution.py:435
  86.9 9.6 %all_to_all.29.cols_ref = bf16[8,8,1152]{2,1,0:T(8,128)(2,1)S(1)} all-to-all(bf16[8,8,1152]{2,1,0:T(8,128)(2,1)} %get-tuple-element.58), channel_id=1, replica_groups=mesh['sec'=8,'proto'=32] {'sec'}, dimensions={0} | all-to-all | bytes 294912 | tf_op jit(solution)/shard_map/all_to_all | solution.py:562
  96.4 0.0 copy-start
  96.4 6.9 %shard_map.59 = bf16[32,16,640]{2,1,0:T(8,128)(2,1)S(1)} custom-call(bf16[512,8192]{1,0:T(8,128)(2,1)S(1)} %get-tuple-element.57.ec_ref, bf16[8,8,1152]{2,1,0:T(8,128)(2,1)S(1)} %all_to_all.29.cols_ref, bf16[512,8192]{1,0:T(8,128)(2,1)S(1)} %get-tuple-element.59.w_ref, bf16[512,512]{1,0:T(8,128)(2,1)} %get-tuple-element.60.u_ref, s32[4,128]{1,0:T(4,128)} %bitcast.8, ...), custom_call_target="tpu_custom_call" | custom-call | flops 4294967296 | bytes 16777216 | tf_op jit(solution)/shard_map/pallas_call | solution.py:435
  103.3 29.0 %all_to_all.30.c_ref = bf16[32,16,640]{2,1,0:T(8,128)(2,1)S(1)} all-to-all(bf16[32,16,640]{2,1,0:T(8,128)(2,1)S(1)} %shard_map.59), channel_id=1, replica_groups=mesh['sec'=8,'proto'=32] {'proto'}, dimensions={0} | all-to-all | bytes 1310720 | tf_op jit(solution)/shard_map/all_to_all | solution.py:478
  132.3 0.0 copy-done
  132.3 0.8 shard_map.60
  (3 shorter events, 0.1 us)
Async XLA Ops:
  0.6 0.7 collective-permute-start.6
  1.4 9.6 %collective-permute-start = (bf16[512,512]{1,0:T(8,128)(2,1)S(1)}, bf16[512,512]{1,0:T(8,128)(2,1)S(1)}, u32[]{:S(2)}, u32[]{:S(2)}) collective-permute-start(bf16[512,512]{1,0:T(8,128)(2,1)S(1)} %get-tuple-element.18.p1_ref), channel_id=1, source_target_pairs={{64,80},{65,81},{66,82},{67,83},{68,84},{69,85},{70,86},{71,87},{7... | collective-permute-start | bytes 1572872 | tf_op jit(solution)/shard_map/cond/branch_0_fun/ppermute | solution.py:523
  2.1 9.8 %slice-start = ((s8[8388608]{0:T(1024)(128)(4,1)}), s8[4194304]{0:T(1024)(128)(4,1)S(1)}, s32[]{:S(2)}) async-start(s8[8388608]{0:T(1024)(128)(4,1)} %bitcast.3), calls=%async_computation.6 | async-start | bytes 8388608 | tf_op jit(solution)/shard_map/cond
  2.1 9.8 %slice-start.1 = ((s8[8388608]{0:T(1024)(128)(4,1)}), s8[4194304]{0:T(1024)(128)(4,1)S(1)}, s32[]{:S(2)}) async-start(s8[8388608]{0:T(1024)(128)(4,1)} %bitcast.3), calls=%async_computation.7 | async-start | bytes 8388608 | tf_op jit(solution)/shard_map/cond
  11.1 0.7 collective-permute-start.1
  21.6 48.4 %all-to-all-start = ((bf16[32,16,640]{2,1,0:T(8,128)(2,1)}), bf16[32,16,640]{2,1,0:T(8,128)(2,1)S(1)}, u32[]{:S(2)}, u32[]{:S(2)}) async-start(bf16[32,16,640]{2,1,0:T(8,128)(2,1)} %branch_0_fun.11), calls=%async_computation | async-start | bytes 1310720 | tf_op jit(solution)/shard_map/cond/branch_0_fun/all_to_all | solution.py:478
  33.2 41.6 %copy-start.1 = (s32[4,128]{1,0:T(4,128)S(1)}, s32[4,128]{1,0:T(4,128)}, u32[]{:S(2)}) copy-start(s32[4,128]{1,0:T(4,128)} %get-tuple-element.29.live_ref) | copy-start | bytes 6148 | tf_op jit(solution)/shard_map/cond
  33.2 42.0 %copy-start.2 = (s32[4,128]{1,0:T(4,128)S(1)}, s32[4,128]{1,0:T(4,128)}, u32[]{:S(2)}) copy-start(s32[4,128]{1,0:T(4,128)} %get-tuple-element.15.index_ref) | copy-start | bytes 6148 | tf_op jit(solution)/shard_map/cond
  33.2 36.8 %collective-permute-start.2 = (bf16[1024,512]{1,0:T(8,128)(2,1)S(1)}, bf16[1024,512]{1,0:T(8,128)(2,1)S(1)}, u32[]{:S(2)}, u32[]{:S(2)}) collective-permute-start(bf16[1024,512]{1,0:T(8,128)(2,1)S(1)} %branch_0_fun.10.both_ref), channel_id=1, source_target_pairs={{64,0},{160,224},{65,1},{161,225},{66,2},{162,226},{67,3},{163,227... | collective-permute-start | bytes 3145736 | tf_op jit(solution)/shard_map/cond/branch_0_fun/ppermute | solution.py:530
  70.0 5.2 %collective-permute-start.3 = (bf16[1024,512]{1,0:T(8,128)(2,1)S(1)}, bf16[1024,512]{1,0:T(8,128)(2,1)S(1)}, u32[]{:S(2)}, u32[]{:S(2)}) collective-permute-start(bf16[1024,512]{1,0:T(8,128)(2,1)S(1)} %collective-permute-done.2.p3_ref), channel_id=1, source_target_pairs={{0,32},{224,192},{1,33},{225,193},{2,34},{226,194},{3,35},{227,195... | collective-permute-start | bytes 3145736 | tf_op jit(solution)/shard_map/cond/branch_0_fun/ppermute | solution.py:538
  96.4 35.9 %copy-start = (s32[512]{0:T(512)S(1)}, s32[512]{0:T(512)}, u32[]{:S(2)}) copy-start(s32[512]{0:T(512)} %param.9) | copy-start | bytes 6148
